TPU v7x, 256 devices: a whole 4x4x8 slice. The times are simulated.
256 devices in a mesh: phase: 64 (over y, z, core), sect: 4 (over x).
Axes of the slice: x: 4, y: 4, z: 8, core: 2. Of those that a mesh axis runs over, the one named last changes fastest.
Arguments:
- activations: bfloat16 [8192, 32768], P('phase', 'sect'), may hold values from 0 to 2
- block_tiles: bfloat16 [64, 512, 8, 4096], P('phase', 'sect'), may hold values from -0.25 to 0.25
- sources: int32 [64, 512, 8], P('phase', 'sect'), may hold values from 0 to 511, all different within a row
- layer_bias: float32 [64], P('phase'), may hold values from -0.6 to -0.2
Outputs:
- next_acts: bfloat16 [8192, 32768], P('phase', 'sect')
Inputs may be any that keep to these rules, and one draw needn't show every extreme that they name: `sources`: each row of 8 entries names distinct input blocks.
All inputs are finite; a program needn't handle non-finite values.
Results may differ from a plain program's by a relative error of at most 0.0055.
Values may be sent and summed in bfloat16 or wider, within the bound.
A program may use at most 128 MiB of HBM per device.

v0:
```python
import functools

import jax
import jax.numpy as jnp
from jax import lax
from jax.experimental import pallas as pl
from jax.experimental.pallas import tpu as pltpu
from jax.sharding import PartitionSpec as P

BLK = 64
CHUNKS = 2
JB = 8


def from_behind(array, axis, by):
    size = lax.axis_size(axis)
    return lax.ppermute(array, axis, [(i, (i + by) % size) for i in range(size)])


def product_kernel(fanin, src_ref, *refs):
    pieces = refs[:5]
    w_ref, b_ref, o_ref, x_ref, sems = refs[5:]
    g = pl.program_id(0)

    @pl.when(g == 0)
    def _():
        rows, width = pieces[0].shape
        half = rows // 2
        targets = [
            x_ref.at[:, pl.ds(0, width)],
            x_ref.at[:, pl.ds(width, width)],
            x_ref.at[pl.ds(0, half), pl.ds(2 * width, width)],
            x_ref.at[pl.ds(half, half), pl.ds(2 * width, width)],
            x_ref.at[:, pl.ds(3 * width, width)],
        ]
        copies = [pltpu.make_async_copy(p, t, sems.at[i]) for i, (p, t) in enumerate(zip(pieces, targets))]
        for c in copies:
            c.start()
        for c in copies:
            c.wait()

    bias = b_ref[0]
    rows = x_ref.shape[0]
    lane = lax.broadcasted_iota(jnp.int32, (rows, 2 * BLK), 1)
    outs = []
    for jj in range(JB):
        j = g * JB + jj
        pairs = []
        for m in range(fanin // 2):
            halves = []
            for h in range(2):
                s = src_ref[j * fanin + 2 * m + h]
                start = pl.multiple_of((s // 2) * (2 * BLK), 2 * BLK)
                x = x_ref[:, pl.ds(start, 2 * BLK)]
                swapped = pltpu.roll(x, BLK, 1)
                keep = (s % 2) == h
                halves.append(jnp.where(keep, x, swapped))
            pairs.append(jnp.where(lane < BLK, halves[0], halves[1]))
        a = jnp.concatenate(pairs, axis=1)
        tiles = w_ref[jj].reshape(fanin, BLK // 2, 2 * BLK)
        parts = []
        for k in range(fanin):
            parts.append(tiles[k][:, :BLK])
            parts.append(pltpu.roll(tiles[k], BLK, 1)[:, :BLK])
        acc = jnp.dot(a, jnp.concatenate(parts, axis=0), preferred_element_type=jnp.float32)
        outs.append(jnp.maximum(acc + bias, 0.0).astype(o_ref.dtype))
    o_ref[...] = jnp.concatenate(outs, axis=1)


def block_layer(pieces, weights, src_flat, layer_bias):
    rows, quarter_width = pieces[0].shape
    width = 4 * quarter_width
    nblk, fanin, _ = weights.shape
    depth = fanin * BLK
    return pl.pallas_call(
        functools.partial(product_kernel, fanin),
        grid_spec=pltpu.PrefetchScalarGridSpec(
            num_scalar_prefetch=1,
            grid=(nblk // JB,),
            in_specs=[
                *[pl.BlockSpec(memory_space=pl.ANY)] * 5,
                pl.BlockSpec((JB, fanin, BLK * BLK), lambda g, s: (g, 0, 0)),
                pl.BlockSpec(memory_space=pltpu.SMEM),
            ],
            out_specs=pl.BlockSpec((rows, JB * BLK), lambda g, s: (0, g)),
            scratch_shapes=[pltpu.VMEM((rows, width), jnp.bfloat16), pltpu.SemaphoreType.DMA((5,))],
        ),
        out_shape=jax.ShapeDtypeStruct((rows, nblk * BLK), jnp.bfloat16),
        compiler_params=pltpu.CompilerParams(vmem_limit_bytes=48 * 1024 * 1024),
        cost_estimate=pl.CostEstimate(
            flops=2 * nblk * depth * 256 * 256,
            bytes_accessed=2 * (weights.size + rows * width + rows * nblk * BLK),
            transcendentals=0,
        ),
    )(src_flat, *pieces, weights, layer_bias)


def gather_sect(quarter):
    from_left = from_behind(quarter, "sect", 1)
    from_right = from_behind(quarter, "sect", -1)
    half = quarter.shape[0] // 2
    opposite_first = from_behind(from_left[:half], "sect", 1)
    opposite_second = from_behind(from_right[half:], "sect", -1)
    return (quarter, from_right, opposite_first, opposite_second, from_left)


def split_parity(quarter):
    pos = jnp.arange(2 * BLK)
    dest = (pos // BLK) * BLK + (pos % 2) * (BLK // 2) + (pos % BLK) // 2
    perm = (dest[:, None] == pos[None, :]).astype(quarter.dtype)
    rows = quarter.shape[0]
    tiles = quarter.reshape(rows, -1, 2 * BLK)
    moved = jnp.einsum("rci,io->rco", tiles, perm, preferred_element_type=jnp.float32)
    return moved.astype(quarter.dtype).reshape(rows, -1)


def layer(quarter, weights, src_flat, layer_bias):
    return block_layer(gather_sect(split_parity(quarter)), weights, src_flat, layer_bias)


def per_device(activations, block_tiles, sources, layer_bias):
    nblk, fanin = sources.shape[1], sources.shape[2]
    weights = block_tiles[0]
    per_quarter = activations.shape[1] // BLK
    size = lax.axis_size("sect")
    me = lax.axis_index("sect")
    src = sources[0].reshape(-1)
    src_flat = ((src // per_quarter - me) % size) * per_quarter + src % per_quarter
    rows = activations.shape[0] // CHUNKS
    outs = []
    for c in range(CHUNKS):
        part = activations[c * rows:(c + 1) * rows]
        hidden = layer(part, weights, src_flat, layer_bias)
        moved = from_behind(hidden, "phase", 1)
        hidden = layer(moved, weights, src_flat, layer_bias)
        outs.append(from_behind(hidden, "phase", 1))
    return jnp.concatenate(outs, axis=0)


def solution(mesh):
    in_specs = (
        P("phase", "sect"),
        P("phase", "sect", None, None),
        P("phase", "sect", None),
        P("phase"),
    )
    out_specs = P("phase", "sect")
    return jax.shard_map(
        per_device, mesh=mesh, in_specs=in_specs, out_specs=out_specs, check_vma=False
    )
```

profile of v0, /device:TPU:6, one launch (start us, length us, event | category | flops | bytes accessed | tf_op | source)
XLA Modules:
  0.0 222.7 jit_solution(12721119593919646930)
XLA Ops:
  0.0 1.7 slice_bitcast_fusion.1
  1.7 0.3 copy.10
  2.0 0.5 convolution_convert_fusion.1
  2.5 0.7 copy.19
  3.2 2.3 %collective-permute-start.11 = (bf16[64,8192]{1,0:T(8,128)(2,1)S(1)}, bf16[64,8192]{1,0:T(8,128)(2,1)S(1)}, u32[]{:S(2)}, u32[]{:S(2)}) collective-permute-start(bf16[64,8192]{1,0:T(8,128)(2,1)S(1)} %bitcast.42), channel_id=1, source_target_pairs={{0,1},{1,2},{2,3},{3,0},{4,5},{5,6},{6,7},{7,4},{8,9},{9,10},{10,1... | collective-permute-start | bytes 3145736 | tf_op jit(solution)/shard_map/ppermute | solution.py:17
  5.5 0.3 copy.6
  5.8 0.5 convolution_convert_fusion.3
  6.3 0.7 copy.21
  7.0 3.3 %collective-permute-start.1 = (bf16[64,8192]{1,0:T(8,128)(2,1)S(1)}, bf16[64,8192]{1,0:T(8,128)(2,1)S(1)}, u32[]{:S(2)}, u32[]{:S(2)}) collective-permute-start(bf16[64,8192]{1,0:T(8,128)(2,1)S(1)} %bitcast.39), channel_id=1, source_target_pairs={{0,1},{1,2},{2,3},{3,0},{4,5},{5,6},{6,7},{7,4},{8,9},{9,10},{10,1... | collective-permute-start | bytes 3145736 | tf_op jit(solution)/shard_map/ppermute | solution.py:17
  10.3 19.0 %collective-permute-done.11.refs_4_ = bf16[64,8192]{1,0:T(8,128)(2,1)S(1)} collective-permute-done((bf16[64,8192]{1,0:T(8,128)(2,1)S(1)}, bf16[64,8192]{1,0:T(8,128)(2,1)S(1)}, u32[]{:S(2)}, u32[]{:S(2)}) %collective-permute-start.11) | collective-permute-done | bytes 1048608 | tf_op jit(solution)/shard_map/ppermute | solution.py:17
  29.3 0.9 slice.44
  30.2 3.5 %collective-permute-start.12 = (bf16[32,8192]{1,0:T(8,128)(2,1)}, bf16[32,8192]{1,0:T(8,128)(2,1)}, u32[]{:S(2)}, u32[]{:S(2)}) collective-permute-start(bf16[32,8192]{1,0:T(8,128)(2,1)} %slice.44), channel_id=1, source_target_pairs={{0,1},{1,2},{2,3},{3,0},{4,5},{5,6},{6,7},{7,4},{8,9},{9,10},{10,1... | collective-permute-start | bytes 1572872 | tf_op jit(solution)/shard_map/ppermute | solution.py:17
  33.7 0.9 slice.45
  34.6 0.3 copy-done.2
  35.5 0.1 copy.5
  35.6 0.1 reshape_squeeze.3
  35.7 16.1 %collective-permute-done.1.refs_4_ = bf16[64,8192]{1,0:T(8,128)(2,1)S(1)} collective-permute-done((bf16[64,8192]{1,0:T(8,128)(2,1)S(1)}, bf16[64,8192]{1,0:T(8,128)(2,1)S(1)}, u32[]{:S(2)}, u32[]{:S(2)}) %collective-permute-start.1) | collective-permute-done | bytes 1048608 | tf_op jit(solution)/shard_map/ppermute | solution.py:17
  51.8 3.5 %collective-permute-start.2 = (bf16[32,8192]{1,0:T(8,128)(2,1)S(1)}, bf16[32,8192]{1,0:T(8,128)(2,1)S(1)}, u32[]{:S(2)}, u32[]{:S(2)}) collective-permute-start(bf16[32,8192]{1,0:T(8,128)(2,1)S(1)} %slice.40), channel_id=1, source_target_pairs={{0,1},{1,2},{2,3},{3,0},{4,5},{5,6},{6,7},{7,4},{8,9},{9,10},{10,1... | collective-permute-start | bytes 1572872 | tf_op jit(solution)/shard_map/ppermute | solution.py:17
  55.4 1.1 slice.41
  56.5 6.6 %collective-permute-done.12.refs_2_ = bf16[32,8192]{1,0:T(8,128)(2,1)} collective-permute-done((bf16[32,8192]{1,0:T(8,128)(2,1)}, bf16[32,8192]{1,0:T(8,128)(2,1)}, u32[]{:S(2)}, u32[]{:S(2)}) %collective-permute-start.12) | collective-permute-done | bytes 524320 | tf_op jit(solution)/shard_map/ppermute | solution.py:17
  63.1 3.5 %collective-permute-done.13.refs_3_ = bf16[32,8192]{1,0:T(8,128)(2,1)} collective-permute-done((bf16[32,8192]{1,0:T(8,128)(2,1)}, bf16[32,8192]{1,0:T(8,128)(2,1)}, u32[]{:S(2)}, u32[]{:S(2)}) %collective-permute-start.13) | collective-permute-done | bytes 524320 | tf_op jit(solution)/shard_map/ppermute | solution.py:17
  66.6 18.9 %shard_map.48 = bf16[64,8192]{1,0:T(8,128)(2,1)S(1)} custom-call(s32[1024]{0:T(1024)S(1)} %fusion.12.src_ref, bf16[64,8192]{1,0:T(8,128)(2,1)S(1)} %bitcast.44, bf16[64,8192]{1,0:T(8,128)(2,1)S(1)} %copy-done.3, bf16[32,8192]{1,0:T(8,128)(2,1)} %collective-permute-done.12.refs_2_, bf16[32,8192]{1,0:T(8,128)(2,1)} %collective-permute-done.13.refs_3_, ...), custom_call_target="tpu_custom_call" | custom-call | flops 8589934592 | bytes 13631488 | tf_op jit(solution)/shard_map/pallas_call | solution.py:75
  85.6 18.9 %shard_map.46 = bf16[64,8192]{1,0:T(8,128)(2,1)S(1)} custom-call(s32[1024]{0:T(1024)S(1)} %fusion.12.src_ref, bf16[64,8192]{1,0:T(8,128)(2,1)S(1)} %bitcast.41, bf16[64,8192]{1,0:T(8,128)(2,1)} %collective-permute-done.refs_1_, bf16[32,8192]{1,0:T(8,128)(2,1)S(1)} %collective-permute-done.2.refs_2_, bf16[32,8192]{1,0:T(8,128)(2,1)S(1)} %collective-permute-done.3.refs_3_, ...), custom_call_target="tpu_custom_call" | custom-call | flops 8589934592 | bytes 13631488 | tf_op jit(solution)/shard_map/pallas_call | solution.py:75
  104.5 0.5 collective-permute-start.4
  105.0 0.3 copy.12
  105.3 0.5 convolution_convert_fusion
  105.8 0.7 copy.18
  106.5 0.4 collective-permute-start.16
  106.8 1.7 collective-permute-start.15
  108.6 13.7 %collective-permute-done.4 = bf16[64,8192]{1,0:T(8,128)(2,1)S(1)} collective-permute-done((bf16[64,8192]{1,0:T(8,128)(2,1)S(1)}, bf16[64,8192]{1,0:T(8,128)(2,1)S(1)}, u32[]{:S(2)}, u32[]{:S(2)}) %collective-permute-start.4) | collective-permute-done | bytes 1048608 | tf_op jit(solution)/shard_map/ppermute | solution.py:17
  122.3 0.3 copy.8
  122.5 0.5 convolution_convert_fusion.2
  123.0 0.7 copy.20
  123.7 0.1 collective-permute-start.6
  123.9 2.0 collective-permute-start.5
  125.8 6.7 %collective-permute-done.16.refs_4_ = bf16[64,8192]{1,0:T(8,128)(2,1)S(1)} collective-permute-done((bf16[64,8192]{1,0:T(8,128)(2,1)S(1)}, bf16[64,8192]{1,0:T(8,128)(2,1)S(1)}, u32[]{:S(2)}, u32[]{:S(2)}) %collective-permute-start.16) | collective-permute-done | bytes 1048608 | tf_op jit(solution)/shard_map/ppermute | solution.py:17
  132.6 1.6 collective-permute-start.17
  134.2 0.6 collective-permute-start.18
  134.8 20.2 %collective-permute-done.6.refs_4_ = bf16[64,8192]{1,0:T(8,128)(2,1)S(1)} collective-permute-done((bf16[64,8192]{1,0:T(8,128)(2,1)S(1)}, bf16[64,8192]{1,0:T(8,128)(2,1)S(1)}, u32[]{:S(2)}, u32[]{:S(2)}) %collective-permute-start.6) | collective-permute-done | bytes 1048608 | tf_op jit(solution)/shard_map/ppermute | solution.py:17
  155.1 1.6 collective-permute-start.7
  156.7 0.6 collective-permute-start.8
  157.3 9.0 %collective-permute-done.17.refs_2_ = bf16[32,8192]{1,0:T(8,128)(2,1)S(1)} collective-permute-done((bf16[32,8192]{1,0:T(8,128)(2,1)S(1)}, bf16[32,8192]{1,0:T(8,128)(2,1)S(1)}, u32[]{:S(2)}, u32[]{:S(2)}) %collective-permute-start.17) | collective-permute-done | bytes 524320 | tf_op jit(solution)/shard_map/ppermute | solution.py:17
  166.3 1.5 collective-permute-done.18.refs_3_
  167.8 17.8 %shard_map.49 = bf16[64,8192]{1,0:T(8,128)(2,1)S(1)} custom-call(s32[1024]{0:T(1024)S(1)} %fusion.12.src_ref, bf16[64,8192]{1,0:T(8,128)(2,1)S(1)} %bitcast.50, bf16[64,8192]{1,0:T(8,128)(2,1)S(1)} %collective-permute-done.15.refs_1_, bf16[32,8192]{1,0:T(8,128)(2,1)S(1)} %collective-permute-done.17.refs_2_, ...), custom_call_target="tpu_custom_call" | custom-call | flops 8589934592 | bytes 13631488 | tf_op jit(solution)/shard_map/pallas_call | solution.py:75
  185.7 17.8 %shard_map.47 = bf16[64,8192]{1,0:T(8,128)(2,1)S(1)} custom-call(s32[1024]{0:T(1024)S(1)} %fusion.12.src_ref, bf16[64,8192]{1,0:T(8,128)(2,1)S(1)} %bitcast.47, bf16[64,8192]{1,0:T(8,128)(2,1)S(1)} %collective-permute-done.5.refs_1_, bf16[32,8192]{1,0:T(8,128)(2,1)S(1)} %collective-permute-done.7.refs_2_, ...), custom_call_target="tpu_custom_call" | custom-call | flops 8589934592 | bytes 13631488 | tf_op jit(solution)/shard_map/pallas_call | solution.py:75
  203.6 2.1 collective-permute-start.9
  205.7 15.5 %collective-permute-done.9 = bf16[64,8192]{1,0:T(8,128)(2,1)S(1)} collective-permute-done((bf16[64,8192]{1,0:T(8,128)(2,1)S(1)}, bf16[64,8192]{1,0:T(8,128)(2,1)S(1)}, u32[]{:S(2)}, u32[]{:S(2)}) %collective-permute-start.9) | collective-permute-done | bytes 1048608 | tf_op jit(solution)/shard_map/ppermute | solution.py:17
  221.2 1.5 pad_maximum_fusion
  (32 shorter events, 0.5 us)
Async XLA Ops:
  3.2 26.1 %collective-permute-start.11 = (bf16[64,8192]{1,0:T(8,128)(2,1)S(1)}, bf16[64,8192]{1,0:T(8,128)(2,1)S(1)}, u32[]{:S(2)}, u32[]{:S(2)}) collective-permute-start(bf16[64,8192]{1,0:T(8,128)(2,1)S(1)} %bitcast.42), channel_id=1, source_target_pairs={{0,1},{1,2},{2,3},{3,0},{4,5},{5,6},{6,7},{7,4},{8,9},{9,10},{10,1... | collective-permute-start | bytes 3145736 | tf_op jit(solution)/shard_map/ppermute | solution.py:17
  5.5 28.2 %collective-permute-start.10 = (bf16[64,8192]{1,0:T(8,128)(2,1)S(1)}, bf16[64,8192]{1,0:T(8,128)(2,1)S(1)}, u32[]{:S(2)}, u32[]{:S(2)}) collective-permute-start(bf16[64,8192]{1,0:T(8,128)(2,1)S(1)} %bitcast.43), channel_id=1, source_target_pairs={{0,3},{1,0},{2,1},{3,2},{4,7},{5,4},{6,5},{7,6},{8,11},{9,8},{10,9... | collective-permute-start | bytes 3145736 | tf_op jit(solution)/shard_map/ppermute | solution.py:17
  6.3 29.2 %copy-start.4 = (s32[1,128,8]{1,2,0:T(8,128)S(1)}, s32[1,128,8]{1,2,0:T(8,128)}, u32[]{:S(2)}) copy-start(s32[1,128,8]{1,2,0:T(8,128)} %param.6) | copy-start | bytes 12292
  7.0 44.8 %collective-permute-start.1 = (bf16[64,8192]{1,0:T(8,128)(2,1)S(1)}, bf16[64,8192]{1,0:T(8,128)(2,1)S(1)}, u32[]{:S(2)}, u32[]{:S(2)}) collective-permute-start(bf16[64,8192]{1,0:T(8,128)(2,1)S(1)} %bitcast.39), channel_id=1, source_target_pairs={{0,1},{1,2},{2,3},{3,0},{4,5},{5,6},{6,7},{7,4},{8,9},{9,10},{10,1... | collective-permute-start | bytes 3145736 | tf_op jit(solution)/shard_map/ppermute | solution.py:17
  10.3 45.1 %collective-permute-start = (bf16[64,8192]{1,0:T(8,128)(2,1)S(1)}, bf16[64,8192]{1,0:T(8,128)(2,1)}, u32[]{:S(2)}, u32[]{:S(2)}) collective-permute-start(bf16[64,8192]{1,0:T(8,128)(2,1)S(1)} %bitcast.40), channel_id=1, source_target_pairs={{0,3},{1,0},{2,1},{3,2},{4,7},{5,4},{6,5},{7,6},{8,11},{9,8},{10,9... | collective-permute-start | bytes 3145736 | tf_op jit(solution)/shard_map/ppermute | solution.py:17
  29.3 4.4 %copy-start = (bf16[64,8192]{1,0:T(8,128)(2,1)}, bf16[64,8192]{1,0:T(8,128)(2,1)S(1)}, u32[]{:S(2)}) copy-start(bf16[64,8192]{1,0:T(8,128)(2,1)S(1)} %collective-permute-done.11.refs_4_) | copy-start | bytes 3145732
  30.2 32.9 %collective-permute-start.12 = (bf16[32,8192]{1,0:T(8,128)(2,1)}, bf16[32,8192]{1,0:T(8,128)(2,1)}, u32[]{:S(2)}, u32[]{:S(2)}) collective-permute-start(bf16[32,8192]{1,0:T(8,128)(2,1)} %slice.44), channel_id=1, source_target_pairs={{0,1},{1,2},{2,3},{3,0},{4,5},{5,6},{6,7},{7,4},{8,9},{9,10},{10,1... | collective-permute-start | bytes 1572872 | tf_op jit(solution)/shard_map/ppermute | solution.py:17
  33.7 1.1 copy-start.2
  34.8 31.8 %collective-permute-start.13 = (bf16[32,8192]{1,0:T(8,128)(2,1)}, bf16[32,8192]{1,0:T(8,128)(2,1)}, u32[]{:S(2)}, u32[]{:S(2)}) collective-permute-start(bf16[32,8192]{1,0:T(8,128)(2,1)} %slice.45), channel_id=1, source_target_pairs={{0,3},{1,0},{2,1},{3,2},{4,7},{5,4},{6,5},{7,6},{8,11},{9,8},{10,9... | collective-permute-start | bytes 1572872 | tf_op jit(solution)/shard_map/ppermute | solution.py:17
  35.7 30.9 %copy-start.1 = (bf16[64,8192]{1,0:T(8,128)(2,1)S(1)}, bf16[64,8192]{1,0:T(8,128)(2,1)}, u32[]{:S(2)}) copy-start(bf16[64,8192]{1,0:T(8,128)(2,1)} %copy-done) | copy-start | bytes 3145732
  35.7 30.9 %copy-start.3 = (bf16[64,8192]{1,0:T(8,128)(2,1)S(1)}, bf16[64,8192]{1,0:T(8,128)(2,1)}, u32[]{:S(2)}) copy-start(bf16[64,8192]{1,0:T(8,128)(2,1)} %copy-done.2) | copy-start | bytes 3145732
  51.8 33.8 %collective-permute-start.2 = (bf16[32,8192]{1,0:T(8,128)(2,1)S(1)}, bf16[32,8192]{1,0:T(8,128)(2,1)S(1)}, u32[]{:S(2)}, u32[]{:S(2)}) collective-permute-start(bf16[32,8192]{1,0:T(8,128)(2,1)S(1)} %slice.40), channel_id=1, source_target_pairs={{0,1},{1,2},{2,3},{3,0},{4,5},{5,6},{6,7},{7,4},{8,9},{9,10},{10,1... | collective-permute-start | bytes 1572872 | tf_op jit(solution)/shard_map/ppermute | solution.py:17
  56.5 29.1 %collective-permute-start.3 = (bf16[32,8192]{1,0:T(8,128)(2,1)S(1)}, bf16[32,8192]{1,0:T(8,128)(2,1)S(1)}, u32[]{:S(2)}, u32[]{:S(2)}) collective-permute-start(bf16[32,8192]{1,0:T(8,128)(2,1)S(1)} %slice.41), channel_id=1, source_target_pairs={{0,3},{1,0},{2,1},{3,2},{4,7},{5,4},{6,5},{7,6},{8,11},{9,8},{10,9... | collective-permute-start | bytes 1572872 | tf_op jit(solution)/shard_map/ppermute | solution.py:17
  85.5 19.5 %collective-permute-start.14 = (bf16[64,8192]{1,0:T(8,128)(2,1)S(1)}, bf16[64,8192]{1,0:T(8,128)(2,1)S(1)}, u32[]{:S(2)}, u32[]{:S(2)}) collective-permute-start(bf16[64,8192]{1,0:T(8,128)(2,1)S(1)} %shard_map.48), channel_id=1, source_target_pairs={{0,4},{4,8},{8,12},{12,16},{16,20},{20,24},{24,28},{28,32},{32,36}... | collective-permute-start | bytes 3145736 | tf_op jit(solution)/shard_map/ppermute | solution.py:17
  104.5 17.8 %collective-permute-start.4 = (bf16[64,8192]{1,0:T(8,128)(2,1)S(1)}, bf16[64,8192]{1,0:T(8,128)(2,1)S(1)}, u32[]{:S(2)}, u32[]{:S(2)}) collective-permute-start(bf16[64,8192]{1,0:T(8,128)(2,1)S(1)} %shard_map.46), channel_id=1, source_target_pairs={{0,4},{4,8},{8,12},{12,16},{16,20},{20,24},{24,28},{28,32},{32,36}... | collective-permute-start | bytes 3145736 | tf_op jit(solution)/shard_map/ppermute | solution.py:17
  106.5 26.1 %collective-permute-start.16 = (bf16[64,8192]{1,0:T(8,128)(2,1)S(1)}, bf16[64,8192]{1,0:T(8,128)(2,1)S(1)}, u32[]{:S(2)}, u32[]{:S(2)}) collective-permute-start(bf16[64,8192]{1,0:T(8,128)(2,1)S(1)} %bitcast.48), channel_id=1, source_target_pairs={{0,1},{1,2},{2,3},{3,0},{4,5},{5,6},{6,7},{7,4},{8,9},{9,10},{10,1... | collective-permute-start | bytes 3145736 | tf_op jit(solution)/shard_map/ppermute | solution.py:17
  106.8 27.3 %collective-permute-start.15 = (bf16[64,8192]{1,0:T(8,128)(2,1)S(1)}, bf16[64,8192]{1,0:T(8,128)(2,1)S(1)}, u32[]{:S(2)}, u32[]{:S(2)}) collective-permute-start(bf16[64,8192]{1,0:T(8,128)(2,1)S(1)} %bitcast.49), channel_id=1, source_target_pairs={{0,3},{1,0},{2,1},{3,2},{4,7},{5,4},{6,5},{7,6},{8,11},{9,8},{10,9... | collective-permute-start | bytes 3145736 | tf_op jit(solution)/shard_map/ppermute | solution.py:17
  123.7 31.3 %collective-permute-start.6 = (bf16[64,8192]{1,0:T(8,128)(2,1)S(1)}, bf16[64,8192]{1,0:T(8,128)(2,1)S(1)}, u32[]{:S(2)}, u32[]{:S(2)}) collective-permute-start(bf16[64,8192]{1,0:T(8,128)(2,1)S(1)} %bitcast.45), channel_id=1, source_target_pairs={{0,1},{1,2},{2,3},{3,0},{4,5},{5,6},{6,7},{7,4},{8,9},{9,10},{10,1... | collective-permute-start | bytes 3145736 | tf_op jit(solution)/shard_map/ppermute | solution.py:17
  123.9 32.8 %collective-permute-start.5 = (bf16[64,8192]{1,0:T(8,128)(2,1)S(1)}, bf16[64,8192]{1,0:T(8,128)(2,1)S(1)}, u32[]{:S(2)}, u32[]{:S(2)}) collective-permute-start(bf16[64,8192]{1,0:T(8,128)(2,1)S(1)} %bitcast.46), channel_id=1, source_target_pairs={{0,3},{1,0},{2,1},{3,2},{4,7},{5,4},{6,5},{7,6},{8,11},{9,8},{10,9... | collective-permute-start | bytes 3145736 | tf_op jit(solution)/shard_map/ppermute | solution.py:17
  132.6 33.7 %collective-permute-start.17 = (bf16[32,8192]{1,0:T(8,128)(2,1)S(1)}, bf16[32,8192]{1,0:T(8,128)(2,1)S(1)}, u32[]{:S(2)}, u32[]{:S(2)}) collective-permute-start(bf16[32,8192]{1,0:T(8,128)(2,1)S(1)} %slice.46), channel_id=1, source_target_pairs={{0,1},{1,2},{2,3},{3,0},{4,5},{5,6},{6,7},{7,4},{8,9},{9,10},{10,1... | collective-permute-start | bytes 1572872 | tf_op jit(solution)/shard_map/ppermute | solution.py:17
  134.2 33.6 %collective-permute-start.18 = (bf16[32,8192]{1,0:T(8,128)(2,1)S(1)}, bf16[32,8192]{1,0:T(8,128)(2,1)S(1)}, u32[]{:S(2)}, u32[]{:S(2)}) collective-permute-start(bf16[32,8192]{1,0:T(8,128)(2,1)S(1)} %slice.47), channel_id=1, source_target_pairs={{0,3},{1,0},{2,1},{3,2},{4,7},{5,4},{6,5},{7,6},{8,11},{9,8},{10,9... | collective-permute-start | bytes 1572872 | tf_op jit(solution)/shard_map/ppermute | solution.py:17
  155.1 30.7 %collective-permute-start.7 = (bf16[32,8192]{1,0:T(8,128)(2,1)S(1)}, bf16[32,8192]{1,0:T(8,128)(2,1)S(1)}, u32[]{:S(2)}, u32[]{:S(2)}) collective-permute-start(bf16[32,8192]{1,0:T(8,128)(2,1)S(1)} %slice.42), channel_id=1, source_target_pairs={{0,1},{1,2},{2,3},{3,0},{4,5},{5,6},{6,7},{7,4},{8,9},{9,10},{10,1... | collective-permute-start | bytes 1572872 | tf_op jit(solution)/shard_map/ppermute | solution.py:17
  156.7 29.0 %collective-permute-start.8 = (bf16[32,8192]{1,0:T(8,128)(2,1)S(1)}, bf16[32,8192]{1,0:T(8,128)(2,1)S(1)}, u32[]{:S(2)}, u32[]{:S(2)}) collective-permute-start(bf16[32,8192]{1,0:T(8,128)(2,1)S(1)} %slice.43), channel_id=1, source_target_pairs={{0,3},{1,0},{2,1},{3,2},{4,7},{5,4},{6,5},{7,6},{8,11},{9,8},{10,9... | collective-permute-start | bytes 1572872 | tf_op jit(solution)/shard_map/ppermute | solution.py:17
  185.6 20.0 %collective-permute-start.19 = (bf16[64,8192]{1,0:T(8,128)(2,1)S(1)}, bf16[64,8192]{1,0:T(8,128)(2,1)S(1)}, u32[]{:S(2)}, u32[]{:S(2)}) collective-permute-start(bf16[64,8192]{1,0:T(8,128)(2,1)S(1)} %shard_map.49), channel_id=1, source_target_pairs={{0,4},{4,8},{8,12},{12,16},{16,20},{20,24},{24,28},{28,32},{32,36}... | collective-permute-start | bytes 3145736 | tf_op jit(solution)/shard_map/ppermute | solution.py:17
  203.6 17.6 %collective-permute-start.9 = (bf16[64,8192]{1,0:T(8,128)(2,1)S(1)}, bf16[64,8192]{1,0:T(8,128)(2,1)S(1)}, u32[]{:S(2)}, u32[]{:S(2)}) collective-permute-start(bf16[64,8192]{1,0:T(8,128)(2,1)S(1)} %shard_map.47), channel_id=1, source_target_pairs={{0,4},{4,8},{8,12},{12,16},{16,20},{20,24},{24,28},{28,32},{32,36}... | collective-permute-start | bytes 3145736 | tf_op jit(solution)/shard_map/ppermute | solution.py:17
where the time goes:
time: 224 us; the launch traced here: 223 us
  waiting for transfers between devices  112 us (50%)
  Pallas kernels  73.4 us (33%)
  starting transfers between devices  24.1 us (11%)
  local copies, waits for them, and re-layouts  9.02 us (4%)
    ppermute x20, waiting for transfers between devices, from_behind(): lax.ppermute(array, axis, [(i, (i + by) % size) for i in range(size)])  112 us
    pallas_call x4, Pallas kernels, block_layer(): pl.pallas_call(functools.partial(product_kernel, fanin), grid_spec=pltpu....  73.4 us
    ppermute x20, starting transfers between devices, from_behind(): lax.ppermute(array, axis, [(i, (i + by) % size) for i in range(size)])  24.1 us
    unnamed x20, local copies, waits for them, and re-layouts  5.9 us
  transfers between devices with their start and end apart: 20, of which 10 were waited for; matrix products, arithmetic and copies ran while one was open for 3% of the time, Pallas kernels for 33%

commit v1 on v0

--- a/solution.py
+++ b/solution.py
@@ -27,11 +27,11 @@
         rows, width = pieces[0].shape
         half = rows // 2
         targets = [
-            x_ref.at[:, pl.ds(0, width)],
-            x_ref.at[:, pl.ds(width, width)],
+            x_ref.at[pl.ds(0, rows), pl.ds(0, width)],
+            x_ref.at[pl.ds(0, rows), pl.ds(width, width)],
             x_ref.at[pl.ds(0, half), pl.ds(2 * width, width)],
             x_ref.at[pl.ds(half, half), pl.ds(2 * width, width)],
-            x_ref.at[:, pl.ds(3 * width, width)],
+            x_ref.at[pl.ds(0, rows), pl.ds(3 * width, width)],
         ]
         copies = [pltpu.make_async_copy(p, t, sems.at[i]) for i, (p, t) in enumerate(zip(pieces, targets))]
         for c in copies:
@@ -40,7 +40,13 @@
             c.wait()
 
     bias = b_ref[0]
-    rows = x_ref.shape[0]
+    rows = x_ref.shape[0] // 2
+    tiles_per_row = x_ref.shape[1] // (2 * BLK)
+
+    @pl.when(g == 0)
+    def _():
+        x_ref[rows:, :] = pltpu.roll(x_ref[:rows, :], BLK, 1)
+
     lane = lax.broadcasted_iota(jnp.int32, (rows, 2 * BLK), 1)
     outs = []
     for jj in range(JB):
@@ -50,11 +56,10 @@
             halves = []
             for h in range(2):
                 s = src_ref[j * fanin + 2 * m + h]
-                start = pl.multiple_of((s // 2) * (2 * BLK), 2 * BLK)
-                x = x_ref[:, pl.ds(start, 2 * BLK)]
-                swapped = pltpu.roll(x, BLK, 1)
-                keep = (s % 2) == h
-                halves.append(jnp.where(keep, x, swapped))
+                moved = (s + h) % 2
+                tile = (s // 2) * (1 - moved) + (((s + 1) // 2) % tiles_per_row) * moved
+                start = pl.multiple_of(tile * (2 * BLK), 2 * BLK)
+                halves.append(x_ref[pl.ds(pl.multiple_of(moved * rows, 8), rows), pl.ds(start, 2 * BLK)])
             pairs.append(jnp.where(lane < BLK, halves[0], halves[1]))
         a = jnp.concatenate(pairs, axis=1)
         tiles = w_ref[jj].reshape(fanin, BLK // 2, 2 * BLK)
@@ -83,7 +88,7 @@
                 pl.BlockSpec(memory_space=pltpu.SMEM),
             ],
             out_specs=pl.BlockSpec((rows, JB * BLK), lambda g, s: (0, g)),
-            scratch_shapes=[pltpu.VMEM((rows, width), jnp.bfloat16), pltpu.SemaphoreType.DMA((5,))],
+            scratch_shapes=[pltpu.VMEM((2 * rows, width), jnp.bfloat16), pltpu.SemaphoreType.DMA((5,))],
         ),
         out_shape=jax.ShapeDtypeStruct((rows, nblk * BLK), jnp.bfloat16),
         compiler_params=pltpu.CompilerParams(vmem_limit_bytes=48 * 1024 * 1024),

time: 224 us -> 246 us (1.098)
  Pallas kernels: 73.4 us -> 96.4 us
    pallas_call x4, Pallas kernels: 73.4 us -> 96.4 us  [block_layer(): pl.pallas_call(functools.partial(product_kernel, fanin), grid_spec=pltpu....]
  transfers between devices with their start and end apart: 20 -> 20, of which waited for: 10 -> 10; matrix products, arithmetic and copies ran while one was open for 3% -> 3% of each run, Pallas kernels for 33% -> 39%
where the time goes in v1:
time: 246 us
  waiting for transfers between devices  112 us (46%)
  Pallas kernels  96.4 us (39%)
  starting transfers between devices  24.3 us (10%)
  local copies, waits for them, and re-layouts  9.02 us (4%)
    ppermute x20, waiting for transfers between devices, from_behind(): lax.ppermute(array, axis, [(i, (i + by) % size) for i in range(size)])  112 us
    pallas_call x4, Pallas kernels, block_layer(): pl.pallas_call(functools.partial(product_kernel, fanin), grid_spec=pltpu....  96.4 us
    ppermute x20, starting transfers between devices, from_behind(): lax.ppermute(array, axis, [(i, (i + by) % size) for i in range(size)])  24.3 us
    unnamed x20, local copies, waits for them, and re-layouts  5.9 us
  transfers between devices with their start and end apart: 20, of which 10 were waited for; matrix products, arithmetic and copies ran while one was open for 3% of the time, Pallas kernels for 39%

profile of v1, /device:TPU:6, one launch (start us, length us, event | category | flops | bytes accessed | tf_op | source)
XLA Modules:
  0.0 245.7 jit_solution(15541691189609359539)
XLA Ops:
  0.0 1.7 slice_bitcast_fusion.1
  1.7 0.3 copy.10
  2.0 0.5 convolution_convert_fusion.1
  2.5 0.7 copy.19
  3.2 2.3 collective-permute-start.11
  5.5 0.3 copy.6
  5.8 0.5 convolution_convert_fusion.3
  6.3 0.7 copy.21
  7.0 3.3 %collective-permute-start.1 = (bf16[64,8192]{1,0:T(8,128)(2,1)S(1)}, bf16[64,8192]{1,0:T(8,128)(2,1)S(1)}, u32[]{:S(2)}, u32[]{:S(2)}) collective-permute-start(bf16[64,8192]{1,0:T(8,128)(2,1)S(1)} %bitcast.39), channel_id=1, source_target_pairs={{0,1},{1,2},{2,3},{3,0},{4,5},{5,6},{6,7},{7,4},{8,9},{9,10},{10,1... | collective-permute-start | bytes 3145736 | tf_op jit(solution)/shard_map/ppermute | solution.py:17
  10.3 19.0 %collective-permute-done.11.refs_4_ = bf16[64,8192]{1,0:T(8,128)(2,1)S(1)} collective-permute-done((bf16[64,8192]{1,0:T(8,128)(2,1)S(1)}, bf16[64,8192]{1,0:T(8,128)(2,1)S(1)}, u32[]{:S(2)}, u32[]{:S(2)}) %collective-permute-start.11) | collective-permute-done | bytes 1048608 | tf_op jit(solution)/shard_map/ppermute | solution.py:17
  29.3 0.9 slice.44
  30.2 3.5 %collective-permute-start.12 = (bf16[32,8192]{1,0:T(8,128)(2,1)}, bf16[32,8192]{1,0:T(8,128)(2,1)}, u32[]{:S(2)}, u32[]{:S(2)}) collective-permute-start(bf16[32,8192]{1,0:T(8,128)(2,1)} %slice.44), channel_id=1, source_target_pairs={{0,1},{1,2},{2,3},{3,0},{4,5},{5,6},{6,7},{7,4},{8,9},{9,10},{10,1... | collective-permute-start | bytes 1572872 | tf_op jit(solution)/shard_map/ppermute | solution.py:17
  33.7 0.9 slice.45
  34.6 0.3 copy-done.2
  35.5 0.1 copy.5
  35.7 16.1 %collective-permute-done.1.refs_4_ = bf16[64,8192]{1,0:T(8,128)(2,1)S(1)} collective-permute-done((bf16[64,8192]{1,0:T(8,128)(2,1)S(1)}, bf16[64,8192]{1,0:T(8,128)(2,1)S(1)}, u32[]{:S(2)}, u32[]{:S(2)}) %collective-permute-start.1) | collective-permute-done | bytes 1048608 | tf_op jit(solution)/shard_map/ppermute | solution.py:17
  51.8 3.5 %collective-permute-start.2 = (bf16[32,8192]{1,0:T(8,128)(2,1)S(1)}, bf16[32,8192]{1,0:T(8,128)(2,1)S(1)}, u32[]{:S(2)}, u32[]{:S(2)}) collective-permute-start(bf16[32,8192]{1,0:T(8,128)(2,1)S(1)} %slice.40), channel_id=1, source_target_pairs={{0,1},{1,2},{2,3},{3,0},{4,5},{5,6},{6,7},{7,4},{8,9},{9,10},{10,1... | collective-permute-start | bytes 1572872 | tf_op jit(solution)/shard_map/ppermute | solution.py:17
  55.4 1.1 slice.41
  56.5 6.6 %collective-permute-done.12.refs_2_ = bf16[32,8192]{1,0:T(8,128)(2,1)} collective-permute-done((bf16[32,8192]{1,0:T(8,128)(2,1)}, bf16[32,8192]{1,0:T(8,128)(2,1)}, u32[]{:S(2)}, u32[]{:S(2)}) %collective-permute-start.12) | collective-permute-done | bytes 524320 | tf_op jit(solution)/shard_map/ppermute | solution.py:17
  63.1 3.5 %collective-permute-done.13.refs_3_ = bf16[32,8192]{1,0:T(8,128)(2,1)} collective-permute-done((bf16[32,8192]{1,0:T(8,128)(2,1)}, bf16[32,8192]{1,0:T(8,128)(2,1)}, u32[]{:S(2)}, u32[]{:S(2)}) %collective-permute-start.13) | collective-permute-done | bytes 524320 | tf_op jit(solution)/shard_map/ppermute | solution.py:17
  66.6 24.6 %shard_map.48 = bf16[64,8192]{1,0:T(8,128)(2,1)S(1)} custom-call(s32[1024]{0:T(1024)S(1)} %fusion.12.src_ref, bf16[64,8192]{1,0:T(8,128)(2,1)S(1)} %bitcast.44, bf16[64,8192]{1,0:T(8,128)(2,1)S(1)} %copy-done.3, bf16[32,8192]{1,0:T(8,128)(2,1)} %collective-permute-done.12.refs_2_, bf16[32,8192]{1,0:T(8,128)(2,1)} %collective-permute-done.13.refs_3_, ...), custom_call_target="tpu_custom_call" | custom-call | flops 8589934592 | bytes 13631488 | tf_op jit(solution)/shard_map/pallas_call | solution.py:80
  91.2 0.3 collective-permute-start.14
  91.5 24.6 %shard_map.46 = bf16[64,8192]{1,0:T(8,128)(2,1)S(1)} custom-call(s32[1024]{0:T(1024)S(1)} %fusion.12.src_ref, bf16[64,8192]{1,0:T(8,128)(2,1)S(1)} %bitcast.41, bf16[64,8192]{1,0:T(8,128)(2,1)} %collective-permute-done.refs_1_, bf16[32,8192]{1,0:T(8,128)(2,1)S(1)} %collective-permute-done.2.refs_2_, bf16[32,8192]{1,0:T(8,128)(2,1)S(1)} %collective-permute-done.3.refs_3_, ...), custom_call_target="tpu_custom_call" | custom-call | flops 8589934592 | bytes 13631488 | tf_op jit(solution)/shard_map/pallas_call | solution.py:80
  116.1 0.3 collective-permute-start.4
  116.5 0.3 copy.12
  116.7 0.5 convolution_convert_fusion
  117.2 0.7 copy.18
  117.9 0.4 collective-permute-start.16
  118.3 1.7 collective-permute-start.15
  120.0 13.7 %collective-permute-done.4 = bf16[64,8192]{1,0:T(8,128)(2,1)S(1)} collective-permute-done((bf16[64,8192]{1,0:T(8,128)(2,1)S(1)}, bf16[64,8192]{1,0:T(8,128)(2,1)S(1)}, u32[]{:S(2)}, u32[]{:S(2)}) %collective-permute-start.4) | collective-permute-done | bytes 1048608 | tf_op jit(solution)/shard_map/ppermute | solution.py:17
  133.8 0.3 copy.8
  134.0 0.5 convolution_convert_fusion.2
  134.5 0.7 copy.20
  135.2 0.1 collective-permute-start.6
  135.3 2.0 collective-permute-start.5
  137.3 6.7 %collective-permute-done.16.refs_4_ = bf16[64,8192]{1,0:T(8,128)(2,1)S(1)} collective-permute-done((bf16[64,8192]{1,0:T(8,128)(2,1)S(1)}, bf16[64,8192]{1,0:T(8,128)(2,1)S(1)}, u32[]{:S(2)}, u32[]{:S(2)}) %collective-permute-start.16) | collective-permute-done | bytes 1048608 | tf_op jit(solution)/shard_map/ppermute | solution.py:17
  144.1 1.6 collective-permute-start.17
  145.7 0.6 collective-permute-start.18
  146.3 20.2 %collective-permute-done.6.refs_4_ = bf16[64,8192]{1,0:T(8,128)(2,1)S(1)} collective-permute-done((bf16[64,8192]{1,0:T(8,128)(2,1)S(1)}, bf16[64,8192]{1,0:T(8,128)(2,1)S(1)}, u32[]{:S(2)}, u32[]{:S(2)}) %collective-permute-start.6) | collective-permute-done | bytes 1048608 | tf_op jit(solution)/shard_map/ppermute | solution.py:17
  166.6 1.6 collective-permute-start.7
  168.2 0.8 collective-permute-start.8
  169.0 8.8 %collective-permute-done.17.refs_2_ = bf16[32,8192]{1,0:T(8,128)(2,1)S(1)} collective-permute-done((bf16[32,8192]{1,0:T(8,128)(2,1)S(1)}, bf16[32,8192]{1,0:T(8,128)(2,1)S(1)}, u32[]{:S(2)}, u32[]{:S(2)}) %collective-permute-start.17) | collective-permute-done | bytes 524320 | tf_op jit(solution)/shard_map/ppermute | solution.py:17
  177.7 1.5 collective-permute-done.18.refs_3_
  179.3 23.6 %shard_map.49 = bf16[64,8192]{1,0:T(8,128)(2,1)S(1)} custom-call(s32[1024]{0:T(1024)S(1)} %fusion.12.src_ref, bf16[64,8192]{1,0:T(8,128)(2,1)S(1)} %bitcast.50, bf16[64,8192]{1,0:T(8,128)(2,1)S(1)} %collective-permute-done.15.refs_1_, bf16[32,8192]{1,0:T(8,128)(2,1)S(1)} %collective-permute-done.17.refs_2_, ...), custom_call_target="tpu_custom_call" | custom-call | flops 8589934592 | bytes 13631488 | tf_op jit(solution)/shard_map/pallas_call | solution.py:80
  203.0 23.6 %shard_map.47 = bf16[64,8192]{1,0:T(8,128)(2,1)S(1)} custom-call(s32[1024]{0:T(1024)S(1)} %fusion.12.src_ref, bf16[64,8192]{1,0:T(8,128)(2,1)S(1)} %bitcast.47, bf16[64,8192]{1,0:T(8,128)(2,1)S(1)} %collective-permute-done.5.refs_1_, bf16[32,8192]{1,0:T(8,128)(2,1)S(1)} %collective-permute-done.7.refs_2_, ...), custom_call_target="tpu_custom_call" | custom-call | flops 8589934592 | bytes 13631488 | tf_op jit(solution)/shard_map/pallas_call | solution.py:80
  226.6 2.1 collective-permute-start.9
  228.6 15.5 %collective-permute-done.9 = bf16[64,8192]{1,0:T(8,128)(2,1)S(1)} collective-permute-done((bf16[64,8192]{1,0:T(8,128)(2,1)S(1)}, bf16[64,8192]{1,0:T(8,128)(2,1)S(1)}, u32[]{:S(2)}, u32[]{:S(2)}) %collective-permute-start.9) | collective-permute-done | bytes 1048608 | tf_op jit(solution)/shard_map/ppermute | solution.py:17
  244.2 1.5 pad_maximum_fusion
  (32 shorter events, 0.5 us)
Async XLA Ops:
  3.2 26.1 %collective-permute-start.11 = (bf16[64,8192]{1,0:T(8,128)(2,1)S(1)}, bf16[64,8192]{1,0:T(8,128)(2,1)S(1)}, u32[]{:S(2)}, u32[]{:S(2)}) collective-permute-start(bf16[64,8192]{1,0:T(8,128)(2,1)S(1)} %bitcast.42), channel_id=1, source_target_pairs={{0,1},{1,2},{2,3},{3,0},{4,5},{5,6},{6,7},{7,4},{8,9},{9,10},{10,1... | collective-permute-start | bytes 3145736 | tf_op jit(solution)/shard_map/ppermute | solution.py:17
  5.5 28.2 %collective-permute-start.10 = (bf16[64,8192]{1,0:T(8,128)(2,1)S(1)}, bf16[64,8192]{1,0:T(8,128)(2,1)S(1)}, u32[]{:S(2)}, u32[]{:S(2)}) collective-permute-start(bf16[64,8192]{1,0:T(8,128)(2,1)S(1)} %bitcast.43), channel_id=1, source_target_pairs={{0,3},{1,0},{2,1},{3,2},{4,7},{5,4},{6,5},{7,6},{8,11},{9,8},{10,9... | collective-permute-start | bytes 3145736 | tf_op jit(solution)/shard_map/ppermute | solution.py:17
  6.3 29.2 %copy-start.4 = (s32[1,128,8]{1,2,0:T(8,128)S(1)}, s32[1,128,8]{1,2,0:T(8,128)}, u32[]{:S(2)}) copy-start(s32[1,128,8]{1,2,0:T(8,128)} %param.6) | copy-start | bytes 12292
  7.0 44.8 %collective-permute-start.1 = (bf16[64,8192]{1,0:T(8,128)(2,1)S(1)}, bf16[64,8192]{1,0:T(8,128)(2,1)S(1)}, u32[]{:S(2)}, u32[]{:S(2)}) collective-permute-start(bf16[64,8192]{1,0:T(8,128)(2,1)S(1)} %bitcast.39), channel_id=1, source_target_pairs={{0,1},{1,2},{2,3},{3,0},{4,5},{5,6},{6,7},{7,4},{8,9},{9,10},{10,1... | collective-permute-start | bytes 3145736 | tf_op jit(solution)/shard_map/ppermute | solution.py:17
  10.3 45.1 %collective-permute-start = (bf16[64,8192]{1,0:T(8,128)(2,1)S(1)}, bf16[64,8192]{1,0:T(8,128)(2,1)}, u32[]{:S(2)}, u32[]{:S(2)}) collective-permute-start(bf16[64,8192]{1,0:T(8,128)(2,1)S(1)} %bitcast.40), channel_id=1, source_target_pairs={{0,3},{1,0},{2,1},{3,2},{4,7},{5,4},{6,5},{7,6},{8,11},{9,8},{10,9... | collective-permute-start | bytes 3145736 | tf_op jit(solution)/shard_map/ppermute | solution.py:17
  29.3 4.4 %copy-start = (bf16[64,8192]{1,0:T(8,128)(2,1)}, bf16[64,8192]{1,0:T(8,128)(2,1)S(1)}, u32[]{:S(2)}) copy-start(bf16[64,8192]{1,0:T(8,128)(2,1)S(1)} %collective-permute-done.11.refs_4_) | copy-start | bytes 3145732
  30.2 32.9 %collective-permute-start.12 = (bf16[32,8192]{1,0:T(8,128)(2,1)}, bf16[32,8192]{1,0:T(8,128)(2,1)}, u32[]{:S(2)}, u32[]{:S(2)}) collective-permute-start(bf16[32,8192]{1,0:T(8,128)(2,1)} %slice.44), channel_id=1, source_target_pairs={{0,1},{1,2},{2,3},{3,0},{4,5},{5,6},{6,7},{7,4},{8,9},{9,10},{10,1... | collective-permute-start | bytes 1572872 | tf_op jit(solution)/shard_map/ppermute | solution.py:17
  33.7 1.1 copy-start.2
  34.8 31.8 %collective-permute-start.13 = (bf16[32,8192]{1,0:T(8,128)(2,1)}, bf16[32,8192]{1,0:T(8,128)(2,1)}, u32[]{:S(2)}, u32[]{:S(2)}) collective-permute-start(bf16[32,8192]{1,0:T(8,128)(2,1)} %slice.45), channel_id=1, source_target_pairs={{0,3},{1,0},{2,1},{3,2},{4,7},{5,4},{6,5},{7,6},{8,11},{9,8},{10,9... | collective-permute-start | bytes 1572872 | tf_op jit(solution)/shard_map/ppermute | solution.py:17
  35.7 30.9 %copy-start.1 = (bf16[64,8192]{1,0:T(8,128)(2,1)S(1)}, bf16[64,8192]{1,0:T(8,128)(2,1)}, u32[]{:S(2)}) copy-start(bf16[64,8192]{1,0:T(8,128)(2,1)} %copy-done) | copy-start | bytes 3145732
  35.7 30.9 %copy-start.3 = (bf16[64,8192]{1,0:T(8,128)(2,1)S(1)}, bf16[64,8192]{1,0:T(8,128)(2,1)}, u32[]{:S(2)}) copy-start(bf16[64,8192]{1,0:T(8,128)(2,1)} %copy-done.2) | copy-start | bytes 3145732
  51.8 39.7 %collective-permute-start.2 = (bf16[32,8192]{1,0:T(8,128)(2,1)S(1)}, bf16[32,8192]{1,0:T(8,128)(2,1)S(1)}, u32[]{:S(2)}, u32[]{:S(2)}) collective-permute-start(bf16[32,8192]{1,0:T(8,128)(2,1)S(1)} %slice.40), channel_id=1, source_target_pairs={{0,1},{1,2},{2,3},{3,0},{4,5},{5,6},{6,7},{7,4},{8,9},{9,10},{10,1... | collective-permute-start | bytes 1572872 | tf_op jit(solution)/shard_map/ppermute | solution.py:17
  56.5 35.1 %collective-permute-start.3 = (bf16[32,8192]{1,0:T(8,128)(2,1)S(1)}, bf16[32,8192]{1,0:T(8,128)(2,1)S(1)}, u32[]{:S(2)}, u32[]{:S(2)}) collective-permute-start(bf16[32,8192]{1,0:T(8,128)(2,1)S(1)} %slice.41), channel_id=1, source_target_pairs={{0,3},{1,0},{2,1},{3,2},{4,7},{5,4},{6,5},{7,6},{8,11},{9,8},{10,9... | collective-permute-start | bytes 1572872 | tf_op jit(solution)/shard_map/ppermute | solution.py:17
  91.2 25.2 %collective-permute-start.14 = (bf16[64,8192]{1,0:T(8,128)(2,1)S(1)}, bf16[64,8192]{1,0:T(8,128)(2,1)S(1)}, u32[]{:S(2)}, u32[]{:S(2)}) collective-permute-start(bf16[64,8192]{1,0:T(8,128)(2,1)S(1)} %shard_map.48), channel_id=1, source_target_pairs={{0,4},{4,8},{8,12},{12,16},{16,20},{20,24},{24,28},{28,32},{32,36}... | collective-permute-start | bytes 3145736 | tf_op jit(solution)/shard_map/ppermute | solution.py:17
  116.1 17.6 %collective-permute-start.4 = (bf16[64,8192]{1,0:T(8,128)(2,1)S(1)}, bf16[64,8192]{1,0:T(8,128)(2,1)S(1)}, u32[]{:S(2)}, u32[]{:S(2)}) collective-permute-start(bf16[64,8192]{1,0:T(8,128)(2,1)S(1)} %shard_map.46), channel_id=1, source_target_pairs={{0,4},{4,8},{8,12},{12,16},{16,20},{20,24},{24,28},{28,32},{32,36}... | collective-permute-start | bytes 3145736 | tf_op jit(solution)/shard_map/ppermute | solution.py:17
  117.9 26.1 %collective-permute-start.16 = (bf16[64,8192]{1,0:T(8,128)(2,1)S(1)}, bf16[64,8192]{1,0:T(8,128)(2,1)S(1)}, u32[]{:S(2)}, u32[]{:S(2)}) collective-permute-start(bf16[64,8192]{1,0:T(8,128)(2,1)S(1)} %bitcast.48), channel_id=1, source_target_pairs={{0,1},{1,2},{2,3},{3,0},{4,5},{5,6},{6,7},{7,4},{8,9},{9,10},{10,1... | collective-permute-start | bytes 3145736 | tf_op jit(solution)/shard_map/ppermute | solution.py:17
  118.3 27.3 %collective-permute-start.15 = (bf16[64,8192]{1,0:T(8,128)(2,1)S(1)}, bf16[64,8192]{1,0:T(8,128)(2,1)S(1)}, u32[]{:S(2)}, u32[]{:S(2)}) collective-permute-start(bf16[64,8192]{1,0:T(8,128)(2,1)S(1)} %bitcast.49), channel_id=1, source_target_pairs={{0,3},{1,0},{2,1},{3,2},{4,7},{5,4},{6,5},{7,6},{8,11},{9,8},{10,9... | collective-permute-start | bytes 3145736 | tf_op jit(solution)/shard_map/ppermute | solution.py:17
  135.2 31.3 %collective-permute-start.6 = (bf16[64,8192]{1,0:T(8,128)(2,1)S(1)}, bf16[64,8192]{1,0:T(8,128)(2,1)S(1)}, u32[]{:S(2)}, u32[]{:S(2)}) collective-permute-start(bf16[64,8192]{1,0:T(8,128)(2,1)S(1)} %bitcast.45), channel_id=1, source_target_pairs={{0,1},{1,2},{2,3},{3,0},{4,5},{5,6},{6,7},{7,4},{8,9},{9,10},{10,1... | collective-permute-start | bytes 3145736 | tf_op jit(solution)/shard_map/ppermute | solution.py:17
  135.3 32.8 %collective-permute-start.5 = (bf16[64,8192]{1,0:T(8,128)(2,1)S(1)}, bf16[64,8192]{1,0:T(8,128)(2,1)S(1)}, u32[]{:S(2)}, u32[]{:S(2)}) collective-permute-start(bf16[64,8192]{1,0:T(8,128)(2,1)S(1)} %bitcast.46), channel_id=1, source_target_pairs={{0,3},{1,0},{2,1},{3,2},{4,7},{5,4},{6,5},{7,6},{8,11},{9,8},{10,9... | collective-permute-start | bytes 3145736 | tf_op jit(solution)/shard_map/ppermute | solution.py:17
  144.1 33.7 %collective-permute-start.17 = (bf16[32,8192]{1,0:T(8,128)(2,1)S(1)}, bf16[32,8192]{1,0:T(8,128)(2,1)S(1)}, u32[]{:S(2)}, u32[]{:S(2)}) collective-permute-start(bf16[32,8192]{1,0:T(8,128)(2,1)S(1)} %slice.46), channel_id=1, source_target_pairs={{0,1},{1,2},{2,3},{3,0},{4,5},{5,6},{6,7},{7,4},{8,9},{9,10},{10,1... | collective-permute-start | bytes 1572872 | tf_op jit(solution)/shard_map/ppermute | solution.py:17
  145.7 33.6 %collective-permute-start.18 = (bf16[32,8192]{1,0:T(8,128)(2,1)S(1)}, bf16[32,8192]{1,0:T(8,128)(2,1)S(1)}, u32[]{:S(2)}, u32[]{:S(2)}) collective-permute-start(bf16[32,8192]{1,0:T(8,128)(2,1)S(1)} %slice.47), channel_id=1, source_target_pairs={{0,3},{1,0},{2,1},{3,2},{4,7},{5,4},{6,5},{7,6},{8,11},{9,8},{10,9... | collective-permute-start | bytes 1572872 | tf_op jit(solution)/shard_map/ppermute | solution.py:17
  166.6 36.4 %collective-permute-start.7 = (bf16[32,8192]{1,0:T(8,128)(2,1)S(1)}, bf16[32,8192]{1,0:T(8,128)(2,1)S(1)}, u32[]{:S(2)}, u32[]{:S(2)}) collective-permute-start(bf16[32,8192]{1,0:T(8,128)(2,1)S(1)} %slice.42), channel_id=1, source_target_pairs={{0,1},{1,2},{2,3},{3,0},{4,5},{5,6},{6,7},{7,4},{8,9},{9,10},{10,1... | collective-permute-start | bytes 1572872 | tf_op jit(solution)/shard_map/ppermute | solution.py:17
  168.2 34.8 %collective-permute-start.8 = (bf16[32,8192]{1,0:T(8,128)(2,1)S(1)}, bf16[32,8192]{1,0:T(8,128)(2,1)S(1)}, u32[]{:S(2)}, u32[]{:S(2)}) collective-permute-start(bf16[32,8192]{1,0:T(8,128)(2,1)S(1)} %slice.43), channel_id=1, source_target_pairs={{0,3},{1,0},{2,1},{3,2},{4,7},{5,4},{6,5},{7,6},{8,11},{9,8},{10,9... | collective-permute-start | bytes 1572872 | tf_op jit(solution)/shard_map/ppermute | solution.py:17
  202.9 25.8 %collective-permute-start.19 = (bf16[64,8192]{1,0:T(8,128)(2,1)S(1)}, bf16[64,8192]{1,0:T(8,128)(2,1)S(1)}, u32[]{:S(2)}, u32[]{:S(2)}) collective-permute-start(bf16[64,8192]{1,0:T(8,128)(2,1)S(1)} %shard_map.49), channel_id=1, source_target_pairs={{0,4},{4,8},{8,12},{12,16},{16,20},{20,24},{24,28},{28,32},{32,36}... | collective-permute-start | bytes 3145736 | tf_op jit(solution)/shard_map/ppermute | solution.py:17
  226.6 17.6 %collective-permute-start.9 = (bf16[64,8192]{1,0:T(8,128)(2,1)S(1)}, bf16[64,8192]{1,0:T(8,128)(2,1)S(1)}, u32[]{:S(2)}, u32[]{:S(2)}) collective-permute-start(bf16[64,8192]{1,0:T(8,128)(2,1)S(1)} %shard_map.47), channel_id=1, source_target_pairs={{0,4},{4,8},{8,12},{12,16},{16,20},{20,24},{24,28},{28,32},{32,36}... | collective-permute-start | bytes 3145736 | tf_op jit(solution)/shard_map/ppermute | solution.py:17

commit v2 on v0

--- a/solution.py
+++ b/solution.py
@@ -9,7 +9,7 @@
 
 BLK = 64
 CHUNKS = 2
-JB = 8
+JB = 16
 
 
 def from_behind(array, axis, by):

time: 224 us -> 215 us (0.960)
  Pallas kernels: 73.4 us -> 64.9 us
    pallas_call x4, Pallas kernels: 73.4 us -> 64.9 us  [block_layer(): pl.pallas_call(functools.partial(product_kernel, fanin), grid_spec=pltpu....]
  transfers between devices with their start and end apart: 20 -> 20, of which waited for: 10 -> 12; matrix products, arithmetic and copies ran while one was open for 3% -> 4% of each run, Pallas kernels for 33% -> 30%
where the time goes in v2:
time: 215 us; the launch traced here: 214 us
  waiting for transfers between devices  112 us (52%)
  Pallas kernels  64.9 us (30%)
  starting transfers between devices  23.9 us (11%)
  local copies, waits for them, and re-layouts  9.02 us (4%)
    ppermute x20, waiting for transfers between devices, from_behind(): lax.ppermute(array, axis, [(i, (i + by) % size) for i in range(size)])  112 us
    pallas_call x4, Pallas kernels, block_layer(): pl.pallas_call(functools.partial(product_kernel, fanin), grid_spec=pltpu....  64.9 us
    ppermute x20, starting transfers between devices, from_behind(): lax.ppermute(array, axis, [(i, (i + by) % size) for i in range(size)])  23.9 us
    unnamed x20, local copies, waits for them, and re-layouts  5.9 us
  transfers between devices with their start and end apart: 20, of which 12 were waited for; matrix products, arithmetic and copies ran while one was open for 4% of the time, Pallas kernels for 30%

profile of v2, /device:TPU:6, one launch (start us, length us, event | category | flops | bytes accessed | tf_op | source)
XLA Modules:
  0.0 214.4 jit_solution(3648717881435714250)
XLA Ops:
  0.0 1.7 slice_bitcast_fusion.1
  1.7 0.3 copy.10
  2.0 0.5 convolution_convert_fusion.1
  2.5 0.7 copy.19
  3.2 2.3 %collective-permute-start.11 = (bf16[64,8192]{1,0:T(8,128)(2,1)S(1)}, bf16[64,8192]{1,0:T(8,128)(2,1)S(1)}, u32[]{:S(2)}, u32[]{:S(2)}) collective-permute-start(bf16[64,8192]{1,0:T(8,128)(2,1)S(1)} %bitcast.42), channel_id=1, source_target_pairs={{0,1},{1,2},{2,3},{3,0},{4,5},{5,6},{6,7},{7,4},{8,9},{9,10},{10,1... | collective-permute-start | bytes 3145736 | tf_op jit(solution)/shard_map/ppermute | solution.py:17
  5.5 0.3 copy.6
  5.8 0.5 convolution_convert_fusion.3
  6.3 0.7 copy.21
  7.0 3.3 %collective-permute-start.1 = (bf16[64,8192]{1,0:T(8,128)(2,1)S(1)}, bf16[64,8192]{1,0:T(8,128)(2,1)S(1)}, u32[]{:S(2)}, u32[]{:S(2)}) collective-permute-start(bf16[64,8192]{1,0:T(8,128)(2,1)S(1)} %bitcast.39), channel_id=1, source_target_pairs={{0,1},{1,2},{2,3},{3,0},{4,5},{5,6},{6,7},{7,4},{8,9},{9,10},{10,1... | collective-permute-start | bytes 3145736 | tf_op jit(solution)/shard_map/ppermute | solution.py:17
  10.3 19.0 %collective-permute-done.11.refs_4_ = bf16[64,8192]{1,0:T(8,128)(2,1)S(1)} collective-permute-done((bf16[64,8192]{1,0:T(8,128)(2,1)S(1)}, bf16[64,8192]{1,0:T(8,128)(2,1)S(1)}, u32[]{:S(2)}, u32[]{:S(2)}) %collective-permute-start.11) | collective-permute-done | bytes 1048608 | tf_op jit(solution)/shard_map/ppermute | solution.py:17
  29.3 0.9 slice.44
  30.2 3.5 %collective-permute-start.12 = (bf16[32,8192]{1,0:T(8,128)(2,1)}, bf16[32,8192]{1,0:T(8,128)(2,1)}, u32[]{:S(2)}, u32[]{:S(2)}) collective-permute-start(bf16[32,8192]{1,0:T(8,128)(2,1)} %slice.44), channel_id=1, source_target_pairs={{0,1},{1,2},{2,3},{3,0},{4,5},{5,6},{6,7},{7,4},{8,9},{9,10},{10,1... | collective-permute-start | bytes 1572872 | tf_op jit(solution)/shard_map/ppermute | solution.py:17
  33.7 0.9 slice.45
  34.6 0.3 copy-done.2
  35.5 0.1 copy.5
  35.6 0.1 reshape_squeeze.3
  35.7 16.1 %collective-permute-done.1.refs_4_ = bf16[64,8192]{1,0:T(8,128)(2,1)S(1)} collective-permute-done((bf16[64,8192]{1,0:T(8,128)(2,1)S(1)}, bf16[64,8192]{1,0:T(8,128)(2,1)S(1)}, u32[]{:S(2)}, u32[]{:S(2)}) %collective-permute-start.1) | collective-permute-done | bytes 1048608 | tf_op jit(solution)/shard_map/ppermute | solution.py:17
  51.8 3.5 %collective-permute-start.2 = (bf16[32,8192]{1,0:T(8,128)(2,1)S(1)}, bf16[32,8192]{1,0:T(8,128)(2,1)S(1)}, u32[]{:S(2)}, u32[]{:S(2)}) collective-permute-start(bf16[32,8192]{1,0:T(8,128)(2,1)S(1)} %slice.40), channel_id=1, source_target_pairs={{0,1},{1,2},{2,3},{3,0},{4,5},{5,6},{6,7},{7,4},{8,9},{9,10},{10,1... | collective-permute-start | bytes 1572872 | tf_op jit(solution)/shard_map/ppermute | solution.py:17
  55.4 1.1 slice.41
  56.5 6.6 %collective-permute-done.12.refs_2_ = bf16[32,8192]{1,0:T(8,128)(2,1)} collective-permute-done((bf16[32,8192]{1,0:T(8,128)(2,1)}, bf16[32,8192]{1,0:T(8,128)(2,1)}, u32[]{:S(2)}, u32[]{:S(2)}) %collective-permute-start.12) | collective-permute-done | bytes 524320 | tf_op jit(solution)/shard_map/ppermute | solution.py:17
  63.1 3.5 %collective-permute-done.13.refs_3_ = bf16[32,8192]{1,0:T(8,128)(2,1)} collective-permute-done((bf16[32,8192]{1,0:T(8,128)(2,1)}, bf16[32,8192]{1,0:T(8,128)(2,1)}, u32[]{:S(2)}, u32[]{:S(2)}) %collective-permute-start.13) | collective-permute-done | bytes 524320 | tf_op jit(solution)/shard_map/ppermute | solution.py:17
  66.6 16.8 %shard_map.48 = bf16[64,8192]{1,0:T(8,128)(2,1)S(1)} custom-call(s32[1024]{0:T(1024)S(1)} %fusion.12.src_ref, bf16[64,8192]{1,0:T(8,128)(2,1)S(1)} %bitcast.44, bf16[64,8192]{1,0:T(8,128)(2,1)S(1)} %copy-done.3, bf16[32,8192]{1,0:T(8,128)(2,1)} %collective-permute-done.12.refs_2_, bf16[32,8192]{1,0:T(8,128)(2,1)} %collective-permute-done.13.refs_3_, ...), custom_call_target="tpu_custom_call" | custom-call | flops 8589934592 | bytes 13631488 | tf_op jit(solution)/shard_map/pallas_call | solution.py:75
  83.4 0.3 collective-permute-start.14
  83.7 16.7 %shard_map.46 = bf16[64,8192]{1,0:T(8,128)(2,1)S(1)} custom-call(s32[1024]{0:T(1024)S(1)} %fusion.12.src_ref, bf16[64,8192]{1,0:T(8,128)(2,1)S(1)} %bitcast.41, bf16[64,8192]{1,0:T(8,128)(2,1)} %collective-permute-done.refs_1_, bf16[32,8192]{1,0:T(8,128)(2,1)S(1)} %collective-permute-done.2.refs_2_, bf16[32,8192]{1,0:T(8,128)(2,1)S(1)} %collective-permute-done.3.refs_3_, ...), custom_call_target="tpu_custom_call" | custom-call | flops 8589934592 | bytes 13631488 | tf_op jit(solution)/shard_map/pallas_call | solution.py:75
  100.4 0.3 collective-permute-start.4
  100.7 0.5 collective-permute-done.14
  101.2 0.3 copy.12
  101.4 0.5 convolution_convert_fusion
  101.9 0.7 copy.18
  102.7 2.0 collective-permute-start.15
  104.7 13.3 %collective-permute-done.4 = bf16[64,8192]{1,0:T(8,128)(2,1)S(1)} collective-permute-done((bf16[64,8192]{1,0:T(8,128)(2,1)S(1)}, bf16[64,8192]{1,0:T(8,128)(2,1)S(1)}, u32[]{:S(2)}, u32[]{:S(2)}) %collective-permute-start.4) | collective-permute-done | bytes 1048608 | tf_op jit(solution)/shard_map/ppermute | solution.py:17
  118.0 0.3 copy.8
  118.3 0.5 convolution_convert_fusion.2
  118.8 0.7 copy.20
  119.6 2.0 collective-permute-start.5
  121.6 7.2 %collective-permute-done.16.refs_4_ = bf16[64,8192]{1,0:T(8,128)(2,1)S(1)} collective-permute-done((bf16[64,8192]{1,0:T(8,128)(2,1)S(1)}, bf16[64,8192]{1,0:T(8,128)(2,1)S(1)}, u32[]{:S(2)}, u32[]{:S(2)}) %collective-permute-start.16) | collective-permute-done | bytes 1048608 | tf_op jit(solution)/shard_map/ppermute | solution.py:17
  128.8 1.3 collective-permute-start.17
  130.1 0.9 collective-permute-start.18
  131.1 20.2 %collective-permute-done.6.refs_4_ = bf16[64,8192]{1,0:T(8,128)(2,1)S(1)} collective-permute-done((bf16[64,8192]{1,0:T(8,128)(2,1)S(1)}, bf16[64,8192]{1,0:T(8,128)(2,1)S(1)}, u32[]{:S(2)}, u32[]{:S(2)}) %collective-permute-start.6) | collective-permute-done | bytes 1048608 | tf_op jit(solution)/shard_map/ppermute | solution.py:17
  151.3 1.2 collective-permute-start.7
  152.6 1.1 collective-permute-start.8
  153.8 8.8 %collective-permute-done.17.refs_2_ = bf16[32,8192]{1,0:T(8,128)(2,1)S(1)} collective-permute-done((bf16[32,8192]{1,0:T(8,128)(2,1)S(1)}, bf16[32,8192]{1,0:T(8,128)(2,1)S(1)}, u32[]{:S(2)}, u32[]{:S(2)}) %collective-permute-start.17) | collective-permute-done | bytes 524320 | tf_op jit(solution)/shard_map/ppermute | solution.py:17
  162.5 1.3 collective-permute-done.18.refs_3_
  163.8 15.7 %shard_map.49 = bf16[64,8192]{1,0:T(8,128)(2,1)S(1)} custom-call(s32[1024]{0:T(1024)S(1)} %fusion.12.src_ref, bf16[64,8192]{1,0:T(8,128)(2,1)S(1)} %bitcast.50, bf16[64,8192]{1,0:T(8,128)(2,1)S(1)} %collective-permute-done.15.refs_1_, bf16[32,8192]{1,0:T(8,128)(2,1)S(1)} %collective-permute-done.17.refs_2_, ...), custom_call_target="tpu_custom_call" | custom-call | flops 8589934592 | bytes 13631488 | tf_op jit(solution)/shard_map/pallas_call | solution.py:75
  179.6 15.7 %shard_map.47 = bf16[64,8192]{1,0:T(8,128)(2,1)S(1)} custom-call(s32[1024]{0:T(1024)S(1)} %fusion.12.src_ref, bf16[64,8192]{1,0:T(8,128)(2,1)S(1)} %bitcast.47, bf16[64,8192]{1,0:T(8,128)(2,1)S(1)} %collective-permute-done.5.refs_1_, bf16[32,8192]{1,0:T(8,128)(2,1)S(1)} %collective-permute-done.7.refs_2_, ...), custom_call_target="tpu_custom_call" | custom-call | flops 8589934592 | bytes 13631488 | tf_op jit(solution)/shard_map/pallas_call | solution.py:75
  195.3 1.8 collective-permute-start.9
  197.1 15.8 %collective-permute-done.9 = bf16[64,8192]{1,0:T(8,128)(2,1)S(1)} collective-permute-done((bf16[64,8192]{1,0:T(8,128)(2,1)S(1)}, bf16[64,8192]{1,0:T(8,128)(2,1)S(1)}, u32[]{:S(2)}, u32[]{:S(2)}) %collective-permute-start.9) | collective-permute-done | bytes 1048608 | tf_op jit(solution)/shard_map/ppermute | solution.py:17
  212.9 1.5 pad_maximum_fusion
  (32 shorter events, 0.7 us)
Async XLA Ops:
  3.2 26.1 %collective-permute-start.11 = (bf16[64,8192]{1,0:T(8,128)(2,1)S(1)}, bf16[64,8192]{1,0:T(8,128)(2,1)S(1)}, u32[]{:S(2)}, u32[]{:S(2)}) collective-permute-start(bf16[64,8192]{1,0:T(8,128)(2,1)S(1)} %bitcast.42), channel_id=1, source_target_pairs={{0,1},{1,2},{2,3},{3,0},{4,5},{5,6},{6,7},{7,4},{8,9},{9,10},{10,1... | collective-permute-start | bytes 3145736 | tf_op jit(solution)/shard_map/ppermute | solution.py:17
  5.5 28.2 %collective-permute-start.10 = (bf16[64,8192]{1,0:T(8,128)(2,1)S(1)}, bf16[64,8192]{1,0:T(8,128)(2,1)S(1)}, u32[]{:S(2)}, u32[]{:S(2)}) collective-permute-start(bf16[64,8192]{1,0:T(8,128)(2,1)S(1)} %bitcast.43), channel_id=1, source_target_pairs={{0,3},{1,0},{2,1},{3,2},{4,7},{5,4},{6,5},{7,6},{8,11},{9,8},{10,9... | collective-permute-start | bytes 3145736 | tf_op jit(solution)/shard_map/ppermute | solution.py:17
  6.3 29.2 %copy-start.4 = (s32[1,128,8]{1,2,0:T(8,128)S(1)}, s32[1,128,8]{1,2,0:T(8,128)}, u32[]{:S(2)}) copy-start(s32[1,128,8]{1,2,0:T(8,128)} %param.6) | copy-start | bytes 12292
  7.0 44.8 %collective-permute-start.1 = (bf16[64,8192]{1,0:T(8,128)(2,1)S(1)}, bf16[64,8192]{1,0:T(8,128)(2,1)S(1)}, u32[]{:S(2)}, u32[]{:S(2)}) collective-permute-start(bf16[64,8192]{1,0:T(8,128)(2,1)S(1)} %bitcast.39), channel_id=1, source_target_pairs={{0,1},{1,2},{2,3},{3,0},{4,5},{5,6},{6,7},{7,4},{8,9},{9,10},{10,1... | collective-permute-start | bytes 3145736 | tf_op jit(solution)/shard_map/ppermute | solution.py:17
  10.3 45.1 %collective-permute-start = (bf16[64,8192]{1,0:T(8,128)(2,1)S(1)}, bf16[64,8192]{1,0:T(8,128)(2,1)}, u32[]{:S(2)}, u32[]{:S(2)}) collective-permute-start(bf16[64,8192]{1,0:T(8,128)(2,1)S(1)} %bitcast.40), channel_id=1, source_target_pairs={{0,3},{1,0},{2,1},{3,2},{4,7},{5,4},{6,5},{7,6},{8,11},{9,8},{10,9... | collective-permute-start | bytes 3145736 | tf_op jit(solution)/shard_map/ppermute | solution.py:17
  29.3 4.4 %copy-start = (bf16[64,8192]{1,0:T(8,128)(2,1)}, bf16[64,8192]{1,0:T(8,128)(2,1)S(1)}, u32[]{:S(2)}) copy-start(bf16[64,8192]{1,0:T(8,128)(2,1)S(1)} %collective-permute-done.11.refs_4_) | copy-start | bytes 3145732
  30.2 32.9 %collective-permute-start.12 = (bf16[32,8192]{1,0:T(8,128)(2,1)}, bf16[32,8192]{1,0:T(8,128)(2,1)}, u32[]{:S(2)}, u32[]{:S(2)}) collective-permute-start(bf16[32,8192]{1,0:T(8,128)(2,1)} %slice.44), channel_id=1, source_target_pairs={{0,1},{1,2},{2,3},{3,0},{4,5},{5,6},{6,7},{7,4},{8,9},{9,10},{10,1... | collective-permute-start | bytes 1572872 | tf_op jit(solution)/shard_map/ppermute | solution.py:17
  33.7 1.1 copy-start.2
  34.8 31.8 %collective-permute-start.13 = (bf16[32,8192]{1,0:T(8,128)(2,1)}, bf16[32,8192]{1,0:T(8,128)(2,1)}, u32[]{:S(2)}, u32[]{:S(2)}) collective-permute-start(bf16[32,8192]{1,0:T(8,128)(2,1)} %slice.45), channel_id=1, source_target_pairs={{0,3},{1,0},{2,1},{3,2},{4,7},{5,4},{6,5},{7,6},{8,11},{9,8},{10,9... | collective-permute-start | bytes 1572872 | tf_op jit(solution)/shard_map/ppermute | solution.py:17
  35.7 30.9 %copy-start.1 = (bf16[64,8192]{1,0:T(8,128)(2,1)S(1)}, bf16[64,8192]{1,0:T(8,128)(2,1)}, u32[]{:S(2)}) copy-start(bf16[64,8192]{1,0:T(8,128)(2,1)} %copy-done) | copy-start | bytes 3145732
  35.7 30.9 %copy-start.3 = (bf16[64,8192]{1,0:T(8,128)(2,1)S(1)}, bf16[64,8192]{1,0:T(8,128)(2,1)}, u32[]{:S(2)}) copy-start(bf16[64,8192]{1,0:T(8,128)(2,1)} %copy-done.2) | copy-start | bytes 3145732
  51.8 31.8 %collective-permute-start.2 = (bf16[32,8192]{1,0:T(8,128)(2,1)S(1)}, bf16[32,8192]{1,0:T(8,128)(2,1)S(1)}, u32[]{:S(2)}, u32[]{:S(2)}) collective-permute-start(bf16[32,8192]{1,0:T(8,128)(2,1)S(1)} %slice.40), channel_id=1, source_target_pairs={{0,1},{1,2},{2,3},{3,0},{4,5},{5,6},{6,7},{7,4},{8,9},{9,10},{10,1... | collective-permute-start | bytes 1572872 | tf_op jit(solution)/shard_map/ppermute | solution.py:17
  56.5 27.2 %collective-permute-start.3 = (bf16[32,8192]{1,0:T(8,128)(2,1)S(1)}, bf16[32,8192]{1,0:T(8,128)(2,1)S(1)}, u32[]{:S(2)}, u32[]{:S(2)}) collective-permute-start(bf16[32,8192]{1,0:T(8,128)(2,1)S(1)} %slice.41), channel_id=1, source_target_pairs={{0,3},{1,0},{2,1},{3,2},{4,7},{5,4},{6,5},{7,6},{8,11},{9,8},{10,9... | collective-permute-start | bytes 1572872 | tf_op jit(solution)/shard_map/ppermute | solution.py:17
  83.4 17.8 %collective-permute-start.14 = (bf16[64,8192]{1,0:T(8,128)(2,1)S(1)}, bf16[64,8192]{1,0:T(8,128)(2,1)S(1)}, u32[]{:S(2)}, u32[]{:S(2)}) collective-permute-start(bf16[64,8192]{1,0:T(8,128)(2,1)S(1)} %shard_map.48), channel_id=1, source_target_pairs={{0,4},{4,8},{8,12},{12,16},{16,20},{20,24},{24,28},{28,32},{32,36}... | collective-permute-start | bytes 3145736 | tf_op jit(solution)/shard_map/ppermute | solution.py:17
  100.4 17.6 %collective-permute-start.4 = (bf16[64,8192]{1,0:T(8,128)(2,1)S(1)}, bf16[64,8192]{1,0:T(8,128)(2,1)S(1)}, u32[]{:S(2)}, u32[]{:S(2)}) collective-permute-start(bf16[64,8192]{1,0:T(8,128)(2,1)S(1)} %shard_map.46), channel_id=1, source_target_pairs={{0,4},{4,8},{8,12},{12,16},{16,20},{20,24},{24,28},{28,32},{32,36}... | collective-permute-start | bytes 3145736 | tf_op jit(solution)/shard_map/ppermute | solution.py:17
  102.6 26.2 %collective-permute-start.16 = (bf16[64,8192]{1,0:T(8,128)(2,1)S(1)}, bf16[64,8192]{1,0:T(8,128)(2,1)S(1)}, u32[]{:S(2)}, u32[]{:S(2)}) collective-permute-start(bf16[64,8192]{1,0:T(8,128)(2,1)S(1)} %bitcast.48), channel_id=1, source_target_pairs={{0,1},{1,2},{2,3},{3,0},{4,5},{5,6},{6,7},{7,4},{8,9},{9,10},{10,1... | collective-permute-start | bytes 3145736 | tf_op jit(solution)/shard_map/ppermute | solution.py:17
  102.7 27.4 %collective-permute-start.15 = (bf16[64,8192]{1,0:T(8,128)(2,1)S(1)}, bf16[64,8192]{1,0:T(8,128)(2,1)S(1)}, u32[]{:S(2)}, u32[]{:S(2)}) collective-permute-start(bf16[64,8192]{1,0:T(8,128)(2,1)S(1)} %bitcast.49), channel_id=1, source_target_pairs={{0,3},{1,0},{2,1},{3,2},{4,7},{5,4},{6,5},{7,6},{8,11},{9,8},{10,9... | collective-permute-start | bytes 3145736 | tf_op jit(solution)/shard_map/ppermute | solution.py:17
  119.5 31.8 %collective-permute-start.6 = (bf16[64,8192]{1,0:T(8,128)(2,1)S(1)}, bf16[64,8192]{1,0:T(8,128)(2,1)S(1)}, u32[]{:S(2)}, u32[]{:S(2)}) collective-permute-start(bf16[64,8192]{1,0:T(8,128)(2,1)S(1)} %bitcast.45), channel_id=1, source_target_pairs={{0,1},{1,2},{2,3},{3,0},{4,5},{5,6},{6,7},{7,4},{8,9},{9,10},{10,1... | collective-permute-start | bytes 3145736 | tf_op jit(solution)/shard_map/ppermute | solution.py:17
  119.6 33.0 %collective-permute-start.5 = (bf16[64,8192]{1,0:T(8,128)(2,1)S(1)}, bf16[64,8192]{1,0:T(8,128)(2,1)S(1)}, u32[]{:S(2)}, u32[]{:S(2)}) collective-permute-start(bf16[64,8192]{1,0:T(8,128)(2,1)S(1)} %bitcast.46), channel_id=1, source_target_pairs={{0,3},{1,0},{2,1},{3,2},{4,7},{5,4},{6,5},{7,6},{8,11},{9,8},{10,9... | collective-permute-start | bytes 3145736 | tf_op jit(solution)/shard_map/ppermute | solution.py:17
  128.8 33.7 %collective-permute-start.17 = (bf16[32,8192]{1,0:T(8,128)(2,1)S(1)}, bf16[32,8192]{1,0:T(8,128)(2,1)S(1)}, u32[]{:S(2)}, u32[]{:S(2)}) collective-permute-start(bf16[32,8192]{1,0:T(8,128)(2,1)S(1)} %slice.46), channel_id=1, source_target_pairs={{0,1},{1,2},{2,3},{3,0},{4,5},{5,6},{6,7},{7,4},{8,9},{9,10},{10,1... | collective-permute-start | bytes 1572872 | tf_op jit(solution)/shard_map/ppermute | solution.py:17
  130.1 33.7 %collective-permute-start.18 = (bf16[32,8192]{1,0:T(8,128)(2,1)S(1)}, bf16[32,8192]{1,0:T(8,128)(2,1)S(1)}, u32[]{:S(2)}, u32[]{:S(2)}) collective-permute-start(bf16[32,8192]{1,0:T(8,128)(2,1)S(1)} %slice.47), channel_id=1, source_target_pairs={{0,3},{1,0},{2,1},{3,2},{4,7},{5,4},{6,5},{7,6},{8,11},{9,8},{10,9... | collective-permute-start | bytes 1572872 | tf_op jit(solution)/shard_map/ppermute | solution.py:17
  151.3 28.3 %collective-permute-start.7 = (bf16[32,8192]{1,0:T(8,128)(2,1)S(1)}, bf16[32,8192]{1,0:T(8,128)(2,1)S(1)}, u32[]{:S(2)}, u32[]{:S(2)}) collective-permute-start(bf16[32,8192]{1,0:T(8,128)(2,1)S(1)} %slice.42), channel_id=1, source_target_pairs={{0,1},{1,2},{2,3},{3,0},{4,5},{5,6},{6,7},{7,4},{8,9},{9,10},{10,1... | collective-permute-start | bytes 1572872 | tf_op jit(solution)/shard_map/ppermute | solution.py:17
  152.6 27.0 %collective-permute-start.8 = (bf16[32,8192]{1,0:T(8,128)(2,1)S(1)}, bf16[32,8192]{1,0:T(8,128)(2,1)S(1)}, u32[]{:S(2)}, u32[]{:S(2)}) collective-permute-start(bf16[32,8192]{1,0:T(8,128)(2,1)S(1)} %slice.43), channel_id=1, source_target_pairs={{0,3},{1,0},{2,1},{3,2},{4,7},{5,4},{6,5},{7,6},{8,11},{9,8},{10,9... | collective-permute-start | bytes 1572872 | tf_op jit(solution)/shard_map/ppermute | solution.py:17
  179.5 17.6 %collective-permute-start.19 = (bf16[64,8192]{1,0:T(8,128)(2,1)S(1)}, bf16[64,8192]{1,0:T(8,128)(2,1)S(1)}, u32[]{:S(2)}, u32[]{:S(2)}) collective-permute-start(bf16[64,8192]{1,0:T(8,128)(2,1)S(1)} %shard_map.49), channel_id=1, source_target_pairs={{0,4},{4,8},{8,12},{12,16},{16,20},{20,24},{24,28},{28,32},{32,36}... | collective-permute-start | bytes 3145736 | tf_op jit(solution)/shard_map/ppermute | solution.py:17
  195.3 17.6 %collective-permute-start.9 = (bf16[64,8192]{1,0:T(8,128)(2,1)S(1)}, bf16[64,8192]{1,0:T(8,128)(2,1)S(1)}, u32[]{:S(2)}, u32[]{:S(2)}) collective-permute-start(bf16[64,8192]{1,0:T(8,128)(2,1)S(1)} %shard_map.47), channel_id=1, source_target_pairs={{0,4},{4,8},{8,12},{12,16},{16,20},{20,24},{24,28},{28,32},{32,36}... | collective-permute-start | bytes 3145736 | tf_op jit(solution)/shard_map/ppermute | solution.py:17

commit v3 on v2

--- a/solution.py
+++ b/solution.py
@@ -9,7 +9,7 @@
 
 BLK = 64
 CHUNKS = 2
-JB = 16
+JB = 32
 
 
 def from_behind(array, axis, by):

time: 215 us -> 213 us (level)
  no operation moved by 1% of the time
where the time goes in v3:
time: 213 us
  waiting for transfers between devices  113 us (53%)
  Pallas kernels  63.5 us (30%)
  starting transfers between devices  23.7 us (11%)
  local copies, waits for them, and re-layouts  9.02 us (4%)
    ppermute x20, waiting for transfers between devices, from_behind(): lax.ppermute(array, axis, [(i, (i + by) % size) for i in range(size)])  113 us
    pallas_call x4, Pallas kernels, block_layer(): pl.pallas_call(functools.partial(product_kernel, fanin), grid_spec=pltpu....  63.5 us
    ppermute x20, starting transfers between devices, from_behind(): lax.ppermute(array, axis, [(i, (i + by) % size) for i in range(size)])  23.7 us
    unnamed x20, local copies, waits for them, and re-layouts  5.9 us
  transfers between devices with their start and end apart: 20, of which 12 were waited for; matrix products, arithmetic and copies ran while one was open for 4% of the time, Pallas kernels for 30%

profile of v3, /device:TPU:6, one launch (start us, length us, event | category | flops | bytes accessed | tf_op | source)
XLA Modules:
  0.0 213.2 jit_solution(6034340804991329243)
XLA Ops:
  0.0 1.7 slice_bitcast_fusion.1
  1.7 0.3 copy.10
  2.0 0.5 convolution_convert_fusion.1
  2.5 0.7 copy.19
  3.2 2.3 %collective-permute-start.11 = (bf16[64,8192]{1,0:T(8,128)(2,1)S(1)}, bf16[64,8192]{1,0:T(8,128)(2,1)S(1)}, u32[]{:S(2)}, u32[]{:S(2)}) collective-permute-start(bf16[64,8192]{1,0:T(8,128)(2,1)S(1)} %bitcast.42), channel_id=1, source_target_pairs={{0,1},{1,2},{2,3},{3,0},{4,5},{5,6},{6,7},{7,4},{8,9},{9,10},{10,1... | collective-permute-start | bytes 3145736 | tf_op jit(solution)/shard_map/ppermute | solution.py:17
  5.5 0.3 copy.6
  5.8 0.5 convolution_convert_fusion.3
  6.3 0.7 copy.21
  7.0 3.3 %collective-permute-start.1 = (bf16[64,8192]{1,0:T(8,128)(2,1)S(1)}, bf16[64,8192]{1,0:T(8,128)(2,1)S(1)}, u32[]{:S(2)}, u32[]{:S(2)}) collective-permute-start(bf16[64,8192]{1,0:T(8,128)(2,1)S(1)} %bitcast.39), channel_id=1, source_target_pairs={{0,1},{1,2},{2,3},{3,0},{4,5},{5,6},{6,7},{7,4},{8,9},{9,10},{10,1... | collective-permute-start | bytes 3145736 | tf_op jit(solution)/shard_map/ppermute | solution.py:17
  10.3 19.0 %collective-permute-done.11.refs_4_ = bf16[64,8192]{1,0:T(8,128)(2,1)S(1)} collective-permute-done((bf16[64,8192]{1,0:T(8,128)(2,1)S(1)}, bf16[64,8192]{1,0:T(8,128)(2,1)S(1)}, u32[]{:S(2)}, u32[]{:S(2)}) %collective-permute-start.11) | collective-permute-done | bytes 1048608 | tf_op jit(solution)/shard_map/ppermute | solution.py:17
  29.3 0.9 slice.44
  30.2 3.5 %collective-permute-start.12 = (bf16[32,8192]{1,0:T(8,128)(2,1)}, bf16[32,8192]{1,0:T(8,128)(2,1)}, u32[]{:S(2)}, u32[]{:S(2)}) collective-permute-start(bf16[32,8192]{1,0:T(8,128)(2,1)} %slice.44), channel_id=1, source_target_pairs={{0,1},{1,2},{2,3},{3,0},{4,5},{5,6},{6,7},{7,4},{8,9},{9,10},{10,1... | collective-permute-start | bytes 1572872 | tf_op jit(solution)/shard_map/ppermute | solution.py:17
  33.7 0.9 slice.45
  34.6 0.3 copy-done.2
  35.7 16.1 %collective-permute-done.1.refs_4_ = bf16[64,8192]{1,0:T(8,128)(2,1)S(1)} collective-permute-done((bf16[64,8192]{1,0:T(8,128)(2,1)S(1)}, bf16[64,8192]{1,0:T(8,128)(2,1)S(1)}, u32[]{:S(2)}, u32[]{:S(2)}) %collective-permute-start.1) | collective-permute-done | bytes 1048608 | tf_op jit(solution)/shard_map/ppermute | solution.py:17
  51.8 3.5 %collective-permute-start.2 = (bf16[32,8192]{1,0:T(8,128)(2,1)S(1)}, bf16[32,8192]{1,0:T(8,128)(2,1)S(1)}, u32[]{:S(2)}, u32[]{:S(2)}) collective-permute-start(bf16[32,8192]{1,0:T(8,128)(2,1)S(1)} %slice.40), channel_id=1, source_target_pairs={{0,1},{1,2},{2,3},{3,0},{4,5},{5,6},{6,7},{7,4},{8,9},{9,10},{10,1... | collective-permute-start | bytes 1572872 | tf_op jit(solution)/shard_map/ppermute | solution.py:17
  55.4 1.1 slice.41
  56.5 0.3 collective-permute-start.3
  56.7 6.4 %collective-permute-done.12.refs_2_ = bf16[32,8192]{1,0:T(8,128)(2,1)} collective-permute-done((bf16[32,8192]{1,0:T(8,128)(2,1)}, bf16[32,8192]{1,0:T(8,128)(2,1)}, u32[]{:S(2)}, u32[]{:S(2)}) %collective-permute-start.12) | collective-permute-done | bytes 524320 | tf_op jit(solution)/shard_map/ppermute | solution.py:17
  63.1 3.5 %collective-permute-done.13.refs_3_ = bf16[32,8192]{1,0:T(8,128)(2,1)} collective-permute-done((bf16[32,8192]{1,0:T(8,128)(2,1)}, bf16[32,8192]{1,0:T(8,128)(2,1)}, u32[]{:S(2)}, u32[]{:S(2)}) %collective-permute-start.13) | collective-permute-done | bytes 524320 | tf_op jit(solution)/shard_map/ppermute | solution.py:17
  66.6 16.5 %shard_map.48 = bf16[64,8192]{1,0:T(8,128)(2,1)S(1)} custom-call(s32[1024]{0:T(1024)S(1)} %fusion.12.src_ref, bf16[64,8192]{1,0:T(8,128)(2,1)S(1)} %bitcast.44, bf16[64,8192]{1,0:T(8,128)(2,1)S(1)} %copy-done.3, bf16[32,8192]{1,0:T(8,128)(2,1)} %collective-permute-done.12.refs_2_, bf16[32,8192]{1,0:T(8,128)(2,1)} %collective-permute-done.13.refs_3_, ...), custom_call_target="tpu_custom_call" | custom-call | flops 8589934592 | bytes 13631488 | tf_op jit(solution)/shard_map/pallas_call | solution.py:75
  83.2 16.5 %shard_map.46 = bf16[64,8192]{1,0:T(8,128)(2,1)S(1)} custom-call(s32[1024]{0:T(1024)S(1)} %fusion.12.src_ref, bf16[64,8192]{1,0:T(8,128)(2,1)S(1)} %bitcast.41, bf16[64,8192]{1,0:T(8,128)(2,1)} %collective-permute-done.refs_1_, bf16[32,8192]{1,0:T(8,128)(2,1)S(1)} %collective-permute-done.2.refs_2_, bf16[32,8192]{1,0:T(8,128)(2,1)S(1)} %collective-permute-done.3.refs_3_, ...), custom_call_target="tpu_custom_call" | custom-call | flops 8589934592 | bytes 13631488 | tf_op jit(solution)/shard_map/pallas_call | solution.py:75
  99.7 0.3 collective-permute-start.4
  100.0 0.7 collective-permute-done.14
  100.7 0.3 copy.12
  101.0 0.5 convolution_convert_fusion
  101.5 0.7 copy.18
  102.3 2.0 collective-permute-start.15
  104.3 13.0 %collective-permute-done.4 = bf16[64,8192]{1,0:T(8,128)(2,1)S(1)} collective-permute-done((bf16[64,8192]{1,0:T(8,128)(2,1)S(1)}, bf16[64,8192]{1,0:T(8,128)(2,1)S(1)}, u32[]{:S(2)}, u32[]{:S(2)}) %collective-permute-start.4) | collective-permute-done | bytes 1048608 | tf_op jit(solution)/shard_map/ppermute | solution.py:17
  117.3 0.3 copy.8
  117.6 0.5 convolution_convert_fusion.2
  118.1 0.7 copy.20
  118.8 0.3 collective-permute-start.6
  119.1 2.0 collective-permute-start.5
  121.1 7.3 %collective-permute-done.16.refs_4_ = bf16[64,8192]{1,0:T(8,128)(2,1)S(1)} collective-permute-done((bf16[64,8192]{1,0:T(8,128)(2,1)S(1)}, bf16[64,8192]{1,0:T(8,128)(2,1)S(1)}, u32[]{:S(2)}, u32[]{:S(2)}) %collective-permute-start.16) | collective-permute-done | bytes 1048608 | tf_op jit(solution)/shard_map/ppermute | solution.py:17
  128.4 1.3 collective-permute-start.17
  129.7 0.9 collective-permute-start.18
  130.6 20.2 %collective-permute-done.6.refs_4_ = bf16[64,8192]{1,0:T(8,128)(2,1)S(1)} collective-permute-done((bf16[64,8192]{1,0:T(8,128)(2,1)S(1)}, bf16[64,8192]{1,0:T(8,128)(2,1)S(1)}, u32[]{:S(2)}, u32[]{:S(2)}) %collective-permute-start.6) | collective-permute-done | bytes 1048608 | tf_op jit(solution)/shard_map/ppermute | solution.py:17
  150.9 1.3 collective-permute-start.7
  152.2 0.9 collective-permute-start.8
  153.1 9.0 %collective-permute-done.17.refs_2_ = bf16[32,8192]{1,0:T(8,128)(2,1)S(1)} collective-permute-done((bf16[32,8192]{1,0:T(8,128)(2,1)S(1)}, bf16[32,8192]{1,0:T(8,128)(2,1)S(1)}, u32[]{:S(2)}, u32[]{:S(2)}) %collective-permute-start.17) | collective-permute-done | bytes 524320 | tf_op jit(solution)/shard_map/ppermute | solution.py:17
  162.1 1.3 collective-permute-done.18.refs_3_
  163.4 15.3 %shard_map.49 = bf16[64,8192]{1,0:T(8,128)(2,1)S(1)} custom-call(s32[1024]{0:T(1024)S(1)} %fusion.12.src_ref, bf16[64,8192]{1,0:T(8,128)(2,1)S(1)} %bitcast.50, bf16[64,8192]{1,0:T(8,128)(2,1)S(1)} %collective-permute-done.15.refs_1_, bf16[32,8192]{1,0:T(8,128)(2,1)S(1)} %collective-permute-done.17.refs_2_, ...), custom_call_target="tpu_custom_call" | custom-call | flops 8589934592 | bytes 13631488 | tf_op jit(solution)/shard_map/pallas_call | solution.py:75
  178.8 15.3 %shard_map.47 = bf16[64,8192]{1,0:T(8,128)(2,1)S(1)} custom-call(s32[1024]{0:T(1024)S(1)} %fusion.12.src_ref, bf16[64,8192]{1,0:T(8,128)(2,1)S(1)} %bitcast.47, bf16[64,8192]{1,0:T(8,128)(2,1)S(1)} %collective-permute-done.5.refs_1_, bf16[32,8192]{1,0:T(8,128)(2,1)S(1)} %collective-permute-done.7.refs_2_, ...), custom_call_target="tpu_custom_call" | custom-call | flops 8589934592 | bytes 13631488 | tf_op jit(solution)/shard_map/pallas_call | solution.py:75
  194.1 1.5 collective-permute-start.9
  195.6 0.6 collective-permute-done.19
  196.3 15.4 %collective-permute-done.9 = bf16[64,8192]{1,0:T(8,128)(2,1)S(1)} collective-permute-done((bf16[64,8192]{1,0:T(8,128)(2,1)S(1)}, bf16[64,8192]{1,0:T(8,128)(2,1)S(1)}, u32[]{:S(2)}, u32[]{:S(2)}) %collective-permute-start.9) | collective-permute-done | bytes 1048608 | tf_op jit(solution)/shard_map/ppermute | solution.py:17
  211.7 1.5 pad_maximum_fusion
  (32 shorter events, 0.7 us)
Async XLA Ops:
  3.2 26.1 %collective-permute-start.11 = (bf16[64,8192]{1,0:T(8,128)(2,1)S(1)}, bf16[64,8192]{1,0:T(8,128)(2,1)S(1)}, u32[]{:S(2)}, u32[]{:S(2)}) collective-permute-start(bf16[64,8192]{1,0:T(8,128)(2,1)S(1)} %bitcast.42), channel_id=1, source_target_pairs={{0,1},{1,2},{2,3},{3,0},{4,5},{5,6},{6,7},{7,4},{8,9},{9,10},{10,1... | collective-permute-start | bytes 3145736 | tf_op jit(solution)/shard_map/ppermute | solution.py:17
  5.5 28.2 %collective-permute-start.10 = (bf16[64,8192]{1,0:T(8,128)(2,1)S(1)}, bf16[64,8192]{1,0:T(8,128)(2,1)S(1)}, u32[]{:S(2)}, u32[]{:S(2)}) collective-permute-start(bf16[64,8192]{1,0:T(8,128)(2,1)S(1)} %bitcast.43), channel_id=1, source_target_pairs={{0,3},{1,0},{2,1},{3,2},{4,7},{5,4},{6,5},{7,6},{8,11},{9,8},{10,9... | collective-permute-start | bytes 3145736 | tf_op jit(solution)/shard_map/ppermute | solution.py:17
  6.3 29.2 %copy-start.4 = (s32[1,128,8]{1,2,0:T(8,128)S(1)}, s32[1,128,8]{1,2,0:T(8,128)}, u32[]{:S(2)}) copy-start(s32[1,128,8]{1,2,0:T(8,128)} %param.6) | copy-start | bytes 12292
  7.0 44.8 %collective-permute-start.1 = (bf16[64,8192]{1,0:T(8,128)(2,1)S(1)}, bf16[64,8192]{1,0:T(8,128)(2,1)S(1)}, u32[]{:S(2)}, u32[]{:S(2)}) collective-permute-start(bf16[64,8192]{1,0:T(8,128)(2,1)S(1)} %bitcast.39), channel_id=1, source_target_pairs={{0,1},{1,2},{2,3},{3,0},{4,5},{5,6},{6,7},{7,4},{8,9},{9,10},{10,1... | collective-permute-start | bytes 3145736 | tf_op jit(solution)/shard_map/ppermute | solution.py:17
  10.3 45.1 %collective-permute-start = (bf16[64,8192]{1,0:T(8,128)(2,1)S(1)}, bf16[64,8192]{1,0:T(8,128)(2,1)}, u32[]{:S(2)}, u32[]{:S(2)}) collective-permute-start(bf16[64,8192]{1,0:T(8,128)(2,1)S(1)} %bitcast.40), channel_id=1, source_target_pairs={{0,3},{1,0},{2,1},{3,2},{4,7},{5,4},{6,5},{7,6},{8,11},{9,8},{10,9... | collective-permute-start | bytes 3145736 | tf_op jit(solution)/shard_map/ppermute | solution.py:17
  29.3 4.4 %copy-start = (bf16[64,8192]{1,0:T(8,128)(2,1)}, bf16[64,8192]{1,0:T(8,128)(2,1)S(1)}, u32[]{:S(2)}) copy-start(bf16[64,8192]{1,0:T(8,128)(2,1)S(1)} %collective-permute-done.11.refs_4_) | copy-start | bytes 3145732
  30.2 32.9 %collective-permute-start.12 = (bf16[32,8192]{1,0:T(8,128)(2,1)}, bf16[32,8192]{1,0:T(8,128)(2,1)}, u32[]{:S(2)}, u32[]{:S(2)}) collective-permute-start(bf16[32,8192]{1,0:T(8,128)(2,1)} %slice.44), channel_id=1, source_target_pairs={{0,1},{1,2},{2,3},{3,0},{4,5},{5,6},{6,7},{7,4},{8,9},{9,10},{10,1... | collective-permute-start | bytes 1572872 | tf_op jit(solution)/shard_map/ppermute | solution.py:17
  33.7 1.1 copy-start.2
  34.8 31.8 %collective-permute-start.13 = (bf16[32,8192]{1,0:T(8,128)(2,1)}, bf16[32,8192]{1,0:T(8,128)(2,1)}, u32[]{:S(2)}, u32[]{:S(2)}) collective-permute-start(bf16[32,8192]{1,0:T(8,128)(2,1)} %slice.45), channel_id=1, source_target_pairs={{0,3},{1,0},{2,1},{3,2},{4,7},{5,4},{6,5},{7,6},{8,11},{9,8},{10,9... | collective-permute-start | bytes 1572872 | tf_op jit(solution)/shard_map/ppermute | solution.py:17
  35.7 30.9 %copy-start.1 = (bf16[64,8192]{1,0:T(8,128)(2,1)S(1)}, bf16[64,8192]{1,0:T(8,128)(2,1)}, u32[]{:S(2)}) copy-start(bf16[64,8192]{1,0:T(8,128)(2,1)} %copy-done) | copy-start | bytes 3145732
  35.7 30.9 %copy-start.3 = (bf16[64,8192]{1,0:T(8,128)(2,1)S(1)}, bf16[64,8192]{1,0:T(8,128)(2,1)}, u32[]{:S(2)}) copy-start(bf16[64,8192]{1,0:T(8,128)(2,1)} %copy-done.2) | copy-start | bytes 3145732
  51.8 31.4 %collective-permute-start.2 = (bf16[32,8192]{1,0:T(8,128)(2,1)S(1)}, bf16[32,8192]{1,0:T(8,128)(2,1)S(1)}, u32[]{:S(2)}, u32[]{:S(2)}) collective-permute-start(bf16[32,8192]{1,0:T(8,128)(2,1)S(1)} %slice.40), channel_id=1, source_target_pairs={{0,1},{1,2},{2,3},{3,0},{4,5},{5,6},{6,7},{7,4},{8,9},{9,10},{10,1... | collective-permute-start | bytes 1572872 | tf_op jit(solution)/shard_map/ppermute | solution.py:17
  56.5 26.7 %collective-permute-start.3 = (bf16[32,8192]{1,0:T(8,128)(2,1)S(1)}, bf16[32,8192]{1,0:T(8,128)(2,1)S(1)}, u32[]{:S(2)}, u32[]{:S(2)}) collective-permute-start(bf16[32,8192]{1,0:T(8,128)(2,1)S(1)} %slice.41), channel_id=1, source_target_pairs={{0,3},{1,0},{2,1},{3,2},{4,7},{5,4},{6,5},{7,6},{8,11},{9,8},{10,9... | collective-permute-start | bytes 1572872 | tf_op jit(solution)/shard_map/ppermute | solution.py:17
  83.1 17.6 %collective-permute-start.14 = (bf16[64,8192]{1,0:T(8,128)(2,1)S(1)}, bf16[64,8192]{1,0:T(8,128)(2,1)S(1)}, u32[]{:S(2)}, u32[]{:S(2)}) collective-permute-start(bf16[64,8192]{1,0:T(8,128)(2,1)S(1)} %shard_map.48), channel_id=1, source_target_pairs={{0,4},{4,8},{8,12},{12,16},{16,20},{20,24},{24,28},{28,32},{32,36}... | collective-permute-start | bytes 3145736 | tf_op jit(solution)/shard_map/ppermute | solution.py:17
  99.7 17.6 %collective-permute-start.4 = (bf16[64,8192]{1,0:T(8,128)(2,1)S(1)}, bf16[64,8192]{1,0:T(8,128)(2,1)S(1)}, u32[]{:S(2)}, u32[]{:S(2)}) collective-permute-start(bf16[64,8192]{1,0:T(8,128)(2,1)S(1)} %shard_map.46), channel_id=1, source_target_pairs={{0,4},{4,8},{8,12},{12,16},{16,20},{20,24},{24,28},{28,32},{32,36}... | collective-permute-start | bytes 3145736 | tf_op jit(solution)/shard_map/ppermute | solution.py:17
  102.2 26.2 %collective-permute-start.16 = (bf16[64,8192]{1,0:T(8,128)(2,1)S(1)}, bf16[64,8192]{1,0:T(8,128)(2,1)S(1)}, u32[]{:S(2)}, u32[]{:S(2)}) collective-permute-start(bf16[64,8192]{1,0:T(8,128)(2,1)S(1)} %bitcast.48), channel_id=1, source_target_pairs={{0,1},{1,2},{2,3},{3,0},{4,5},{5,6},{6,7},{7,4},{8,9},{9,10},{10,1... | collective-permute-start | bytes 3145736 | tf_op jit(solution)/shard_map/ppermute | solution.py:17
  102.3 27.4 %collective-permute-start.15 = (bf16[64,8192]{1,0:T(8,128)(2,1)S(1)}, bf16[64,8192]{1,0:T(8,128)(2,1)S(1)}, u32[]{:S(2)}, u32[]{:S(2)}) collective-permute-start(bf16[64,8192]{1,0:T(8,128)(2,1)S(1)} %bitcast.49), channel_id=1, source_target_pairs={{0,3},{1,0},{2,1},{3,2},{4,7},{5,4},{6,5},{7,6},{8,11},{9,8},{10,9... | collective-permute-start | bytes 3145736 | tf_op jit(solution)/shard_map/ppermute | solution.py:17
  118.8 32.1 %collective-permute-start.6 = (bf16[64,8192]{1,0:T(8,128)(2,1)S(1)}, bf16[64,8192]{1,0:T(8,128)(2,1)S(1)}, u32[]{:S(2)}, u32[]{:S(2)}) collective-permute-start(bf16[64,8192]{1,0:T(8,128)(2,1)S(1)} %bitcast.45), channel_id=1, source_target_pairs={{0,1},{1,2},{2,3},{3,0},{4,5},{5,6},{6,7},{7,4},{8,9},{9,10},{10,1... | collective-permute-start | bytes 3145736 | tf_op jit(solution)/shard_map/ppermute | solution.py:17
  119.1 33.1 %collective-permute-start.5 = (bf16[64,8192]{1,0:T(8,128)(2,1)S(1)}, bf16[64,8192]{1,0:T(8,128)(2,1)S(1)}, u32[]{:S(2)}, u32[]{:S(2)}) collective-permute-start(bf16[64,8192]{1,0:T(8,128)(2,1)S(1)} %bitcast.46), channel_id=1, source_target_pairs={{0,3},{1,0},{2,1},{3,2},{4,7},{5,4},{6,5},{7,6},{8,11},{9,8},{10,9... | collective-permute-start | bytes 3145736 | tf_op jit(solution)/shard_map/ppermute | solution.py:17
  128.4 33.7 %collective-permute-start.17 = (bf16[32,8192]{1,0:T(8,128)(2,1)S(1)}, bf16[32,8192]{1,0:T(8,128)(2,1)S(1)}, u32[]{:S(2)}, u32[]{:S(2)}) collective-permute-start(bf16[32,8192]{1,0:T(8,128)(2,1)S(1)} %slice.46), channel_id=1, source_target_pairs={{0,1},{1,2},{2,3},{3,0},{4,5},{5,6},{6,7},{7,4},{8,9},{9,10},{10,1... | collective-permute-start | bytes 1572872 | tf_op jit(solution)/shard_map/ppermute | solution.py:17
  129.7 33.6 %collective-permute-start.18 = (bf16[32,8192]{1,0:T(8,128)(2,1)S(1)}, bf16[32,8192]{1,0:T(8,128)(2,1)S(1)}, u32[]{:S(2)}, u32[]{:S(2)}) collective-permute-start(bf16[32,8192]{1,0:T(8,128)(2,1)S(1)} %slice.47), channel_id=1, source_target_pairs={{0,3},{1,0},{2,1},{3,2},{4,7},{5,4},{6,5},{7,6},{8,11},{9,8},{10,9... | collective-permute-start | bytes 1572872 | tf_op jit(solution)/shard_map/ppermute | solution.py:17
  150.9 27.9 %collective-permute-start.7 = (bf16[32,8192]{1,0:T(8,128)(2,1)S(1)}, bf16[32,8192]{1,0:T(8,128)(2,1)S(1)}, u32[]{:S(2)}, u32[]{:S(2)}) collective-permute-start(bf16[32,8192]{1,0:T(8,128)(2,1)S(1)} %slice.42), channel_id=1, source_target_pairs={{0,1},{1,2},{2,3},{3,0},{4,5},{5,6},{6,7},{7,4},{8,9},{9,10},{10,1... | collective-permute-start | bytes 1572872 | tf_op jit(solution)/shard_map/ppermute | solution.py:17
  152.2 26.6 %collective-permute-start.8 = (bf16[32,8192]{1,0:T(8,128)(2,1)S(1)}, bf16[32,8192]{1,0:T(8,128)(2,1)S(1)}, u32[]{:S(2)}, u32[]{:S(2)}) collective-permute-start(bf16[32,8192]{1,0:T(8,128)(2,1)S(1)} %slice.43), channel_id=1, source_target_pairs={{0,3},{1,0},{2,1},{3,2},{4,7},{5,4},{6,5},{7,6},{8,11},{9,8},{10,9... | collective-permute-start | bytes 1572872 | tf_op jit(solution)/shard_map/ppermute | solution.py:17
  178.7 17.6 %collective-permute-start.19 = (bf16[64,8192]{1,0:T(8,128)(2,1)S(1)}, bf16[64,8192]{1,0:T(8,128)(2,1)S(1)}, u32[]{:S(2)}, u32[]{:S(2)}) collective-permute-start(bf16[64,8192]{1,0:T(8,128)(2,1)S(1)} %shard_map.49), channel_id=1, source_target_pairs={{0,4},{4,8},{8,12},{12,16},{16,20},{20,24},{24,28},{28,32},{32,36}... | collective-permute-start | bytes 3145736 | tf_op jit(solution)/shard_map/ppermute | solution.py:17
  194.1 17.6 %collective-permute-start.9 = (bf16[64,8192]{1,0:T(8,128)(2,1)S(1)}, bf16[64,8192]{1,0:T(8,128)(2,1)S(1)}, u32[]{:S(2)}, u32[]{:S(2)}) collective-permute-start(bf16[64,8192]{1,0:T(8,128)(2,1)S(1)} %shard_map.47), channel_id=1, source_target_pairs={{0,4},{4,8},{8,12},{12,16},{16,20},{20,24},{24,28},{28,32},{32,36}... | collective-permute-start | bytes 3145736 | tf_op jit(solution)/shard_map/ppermute | solution.py:17

commit v4 on v3

--- a/solution.py
+++ b/solution.py
@@ -128,9 +128,14 @@
     src_flat = ((src // per_quarter - me) % size) * per_quarter + src % per_quarter
     rows = activations.shape[0] // CHUNKS
     outs = []
+    first = gather_sect(split_parity(activations[:rows]))
     for c in range(CHUNKS):
-        part = activations[c * rows:(c + 1) * rows]
-        hidden = layer(part, weights, src_flat, layer_bias)
+        if c == 0:
+            pieces = first
+        else:
+            part, first = lax.optimization_barrier((split_parity(activations[c * rows:(c + 1) * rows]), first))
+            pieces = gather_sect(part)
+        hidden = block_layer(pieces, weights, src_flat, layer_bias)
         moved = from_behind(hidden, "phase", 1)
         hidden = layer(moved, weights, src_flat, layer_bias)
         outs.append(from_behind(hidden, "phase", 1))

time: 213 us -> 223 us (1.047)
  starting transfers between devices: 23.7 us -> 29.4 us
  waiting for transfers between devices: 113 us -> 116 us
    ppermute x20, starting transfers between devices: 23.7 us -> 29.4 us  [from_behind(): lax.ppermute(array, axis, [(i, (i + by) % size) for i in range(size)])]
    ppermute x20, waiting for transfers between devices: 113 us -> 116 us  [from_behind(): lax.ppermute(array, axis, [(i, (i + by) % size) for i in range(size)])]
    unnamed x20 -> x24, local copies, waits for them, and re-layouts: 5.9 us -> 7.24 us
  transfers between devices with their start and end apart: 20 -> 20, of which waited for: 12 -> 11; matrix products, arithmetic and copies ran while one was open for 4% -> 3% of each run, Pallas kernels for 30% -> 28%
where the time goes in v4:
time: 223 us; the launch traced here: 222 us
  waiting for transfers between devices  116 us (52%)
  Pallas kernels  62.7 us (28%)
  starting transfers between devices  29.4 us (13%)
  local copies, waits for them, and re-layouts  9.7 us (4%)
    ppermute x20, waiting for transfers between devices, from_behind(): lax.ppermute(array, axis, [(i, (i + by) % size) for i in range(size)])  116 us
    pallas_call x4, Pallas kernels, block_layer(): pl.pallas_call(functools.partial(product_kernel, fanin), grid_spec=pltpu....  62.7 us
    ppermute x20, starting transfers between devices, from_behind(): lax.ppermute(array, axis, [(i, (i + by) % size) for i in range(size)])  29.4 us
    unnamed x24, local copies, waits for them, and re-layouts  7.24 us
  transfers between devices with their start and end apart: 20, of which 11 were waited for; matrix products, arithmetic and copies ran while one was open for 3% of the time, Pallas kernels for 28%

profile of v4, /device:TPU:6, one launch (start us, length us, event | category | flops | bytes accessed | tf_op | source)
XLA Modules:
  0.0 222.3 jit_solution(11001783929984280523)
XLA Ops:
  0.0 1.7 slice_bitcast_fusion.1
  1.7 0.3 copy.6
  2.0 0.5 convolution_convert_fusion.3
  2.5 0.7 copy.21
  3.2 2.3 %collective-permute-start.1 = (bf16[64,8192]{1,0:T(8,128)(2,1)S(1)}, bf16[64,8192]{1,0:T(8,128)(2,1)S(1)}, u32[]{:S(2)}, u32[]{:S(2)}) collective-permute-start(bf16[64,8192]{1,0:T(8,128)(2,1)S(1)} %bitcast.39), channel_id=1, source_target_pairs={{0,1},{1,2},{2,3},{3,0},{4,5},{5,6},{6,7},{7,4},{8,9},{9,10},{10,1... | collective-permute-start | bytes 3145736 | tf_op jit(solution)/shard_map/ppermute | solution.py:17
  5.5 22.7 %collective-permute-done.1.refs_4_ = bf16[64,8192]{1,0:T(8,128)(2,1)S(1)} collective-permute-done((bf16[64,8192]{1,0:T(8,128)(2,1)S(1)}, bf16[64,8192]{1,0:T(8,128)(2,1)S(1)}, u32[]{:S(2)}, u32[]{:S(2)}) %collective-permute-start.1) | collective-permute-done | bytes 1048608 | tf_op jit(solution)/shard_map/ppermute | solution.py:17
  28.2 1.6 collective-permute-start.2
  29.8 0.6 collective-permute-start.3
  30.4 0.3 copy.10
  30.7 0.5 convolution_convert_fusion.1
  31.2 0.7 copy.19
  31.9 9.1 %collective-permute-done.2.refs_2_ = bf16[32,8192]{1,0:T(8,128)(2,1)S(1)} collective-permute-done((bf16[32,8192]{1,0:T(8,128)(2,1)S(1)}, bf16[32,8192]{1,0:T(8,128)(2,1)S(1)}, u32[]{:S(2)}, u32[]{:S(2)}) %collective-permute-start.2) | collective-permute-done | bytes 524320 | tf_op jit(solution)/shard_map/ppermute | solution.py:17
  41.1 0.8 copy-done.2
  41.9 0.6 collective-permute-done.3.refs_3_
  42.4 0.8 copy-done.4
  43.2 0.9 collective-permute-start.11
  44.2 1.1 collective-permute-start.10
  45.9 0.1 copy.5
  46.0 0.1 reshape_squeeze.3
  46.2 19.7 %collective-permute-done.11.refs_4_ = bf16[64,8192]{1,0:T(8,128)(2,1)} collective-permute-done((bf16[64,8192]{1,0:T(8,128)(2,1)S(1)}, bf16[64,8192]{1,0:T(8,128)(2,1)}, u32[]{:S(2)}, u32[]{:S(2)}) %collective-permute-start.11) | collective-permute-done | bytes 1048608 | tf_op jit(solution)/shard_map/ppermute | solution.py:17
  65.9 1.1 slice.44
  67.0 1.6 collective-permute-start.12
  68.5 1.1 slice.45
  69.6 0.8 collective-permute-start.13
  70.4 15.3 %shard_map.46 = bf16[64,8192]{1,0:T(8,128)(2,1)S(1)} custom-call(s32[1024]{0:T(1024)S(1)} %fusion.12.src_ref, bf16[64,8192]{1,0:T(8,128)(2,1)S(1)} %bitcast.41, bf16[64,8192]{1,0:T(8,128)(2,1)S(1)} %copy-done.1, bf16[32,8192]{1,0:T(8,128)(2,1)S(1)} %copy-done.3, bf16[32,8192]{1,0:T(8,128)(2,1)S(1)} %copy-done.5, ...), custom_call_target="tpu_custom_call" | custom-call | flops 8589934592 | bytes 13631488 | tf_op jit(solution)/shard_map/pallas_call | solution.py:75
  85.8 16.7 %shard_map.48 = bf16[64,8192]{1,0:T(8,128)(2,1)S(1)} custom-call(s32[1024]{0:T(1024)S(1)} %fusion.12.src_ref, bf16[64,8192]{1,0:T(8,128)(2,1)S(1)} %bitcast.50, bf16[64,8192]{1,0:T(8,128)(2,1)} %collective-permute-done.10.refs_1_, bf16[32,8192]{1,0:T(8,128)(2,1)S(1)} %collective-permute-done.12.refs_2_, ...), custom_call_target="tpu_custom_call" | custom-call | flops 8589934592 | bytes 13631488 | tf_op jit(solution)/shard_map/pallas_call | solution.py:75
  102.6 4.2 %collective-permute-start.14 = (bf16[64,8192]{1,0:T(8,128)(2,1)S(1)}, bf16[64,8192]{1,0:T(8,128)(2,1)S(1)}, u32[]{:S(2)}, u32[]{:S(2)}) collective-permute-start(bf16[64,8192]{1,0:T(8,128)(2,1)S(1)} %shard_map.48), channel_id=1, source_target_pairs={{0,4},{4,8},{8,12},{12,16},{16,20},{20,24},{24,28},{28,32},{32,36}... | collective-permute-start | bytes 3145736 | tf_op jit(solution)/shard_map/ppermute | solution.py:17
  106.8 0.3 copy.8
  107.0 0.5 convolution_convert_fusion.2
  107.5 0.7 copy.20
  108.2 3.3 %collective-permute-start.6 = (bf16[64,8192]{1,0:T(8,128)(2,1)S(1)}, bf16[64,8192]{1,0:T(8,128)(2,1)S(1)}, u32[]{:S(2)}, u32[]{:S(2)}) collective-permute-start(bf16[64,8192]{1,0:T(8,128)(2,1)S(1)} %bitcast.45), channel_id=1, source_target_pairs={{0,1},{1,2},{2,3},{3,0},{4,5},{5,6},{6,7},{7,4},{8,9},{9,10},{10,1... | collective-permute-start | bytes 3145736 | tf_op jit(solution)/shard_map/ppermute | solution.py:17
  111.5 10.5 %collective-permute-done.14 = bf16[64,8192]{1,0:T(8,128)(2,1)S(1)} collective-permute-done((bf16[64,8192]{1,0:T(8,128)(2,1)S(1)}, bf16[64,8192]{1,0:T(8,128)(2,1)S(1)}, u32[]{:S(2)}, u32[]{:S(2)}) %collective-permute-start.14) | collective-permute-done | bytes 1048608 | tf_op jit(solution)/shard_map/ppermute | solution.py:17
  122.0 0.3 copy.12
  122.3 0.5 convolution_convert_fusion
  122.8 0.7 copy.18
  123.5 3.2 %collective-permute-start.16 = (bf16[64,8192]{1,0:T(8,128)(2,1)S(1)}, bf16[64,8192]{1,0:T(8,128)(2,1)S(1)}, u32[]{:S(2)}, u32[]{:S(2)}) collective-permute-start(bf16[64,8192]{1,0:T(8,128)(2,1)S(1)} %bitcast.42), channel_id=1, source_target_pairs={{0,1},{1,2},{2,3},{3,0},{4,5},{5,6},{6,7},{7,4},{8,9},{9,10},{10,1... | collective-permute-start | bytes 3145736 | tf_op jit(solution)/shard_map/ppermute | solution.py:17
  126.7 8.4 %collective-permute-done.6.refs_4_ = bf16[64,8192]{1,0:T(8,128)(2,1)S(1)} collective-permute-done((bf16[64,8192]{1,0:T(8,128)(2,1)S(1)}, bf16[64,8192]{1,0:T(8,128)(2,1)S(1)}, u32[]{:S(2)}, u32[]{:S(2)}) %collective-permute-start.6) | collective-permute-done | bytes 1048608 | tf_op jit(solution)/shard_map/ppermute | solution.py:17
  135.1 3.8 %collective-permute-start.7 = (bf16[32,8192]{1,0:T(8,128)(2,1)S(1)}, bf16[32,8192]{1,0:T(8,128)(2,1)S(1)}, u32[]{:S(2)}, u32[]{:S(2)}) collective-permute-start(bf16[32,8192]{1,0:T(8,128)(2,1)S(1)} %slice.42), channel_id=1, source_target_pairs={{0,1},{1,2},{2,3},{3,0},{4,5},{5,6},{6,7},{7,4},{8,9},{9,10},{10,1... | collective-permute-start | bytes 1572872 | tf_op jit(solution)/shard_map/ppermute | solution.py:17
  139.0 18.5 %collective-permute-done.16.refs_4_ = bf16[64,8192]{1,0:T(8,128)(2,1)S(1)} collective-permute-done((bf16[64,8192]{1,0:T(8,128)(2,1)S(1)}, bf16[64,8192]{1,0:T(8,128)(2,1)S(1)}, u32[]{:S(2)}, u32[]{:S(2)}) %collective-permute-start.16) | collective-permute-done | bytes 1048608 | tf_op jit(solution)/shard_map/ppermute | solution.py:17
  157.6 3.8 %collective-permute-start.17 = (bf16[32,8192]{1,0:T(8,128)(2,1)S(1)}, bf16[32,8192]{1,0:T(8,128)(2,1)S(1)}, u32[]{:S(2)}, u32[]{:S(2)}) collective-permute-start(bf16[32,8192]{1,0:T(8,128)(2,1)S(1)} %slice.46), channel_id=1, source_target_pairs={{0,1},{1,2},{2,3},{3,0},{4,5},{5,6},{6,7},{7,4},{8,9},{9,10},{10,1... | collective-permute-start | bytes 1572872 | tf_op jit(solution)/shard_map/ppermute | solution.py:17
  161.5 7.3 %collective-permute-done.7.refs_2_ = bf16[32,8192]{1,0:T(8,128)(2,1)S(1)} collective-permute-done((bf16[32,8192]{1,0:T(8,128)(2,1)S(1)}, bf16[32,8192]{1,0:T(8,128)(2,1)S(1)}, u32[]{:S(2)}, u32[]{:S(2)}) %collective-permute-start.7) | collective-permute-done | bytes 524320 | tf_op jit(solution)/shard_map/ppermute | solution.py:17
  168.8 3.7 %collective-permute-done.8.refs_3_ = bf16[32,8192]{1,0:T(8,128)(2,1)S(1)} collective-permute-done((bf16[32,8192]{1,0:T(8,128)(2,1)S(1)}, bf16[32,8192]{1,0:T(8,128)(2,1)S(1)}, u32[]{:S(2)}, u32[]{:S(2)}) %collective-permute-start.8) | collective-permute-done | bytes 524320 | tf_op jit(solution)/shard_map/ppermute | solution.py:17
  172.5 15.3 %shard_map.47 = bf16[64,8192]{1,0:T(8,128)(2,1)S(1)} custom-call(s32[1024]{0:T(1024)S(1)} %fusion.12.src_ref, bf16[64,8192]{1,0:T(8,128)(2,1)S(1)} %bitcast.47, bf16[64,8192]{1,0:T(8,128)(2,1)S(1)} %collective-permute-done.5.refs_1_, bf16[32,8192]{1,0:T(8,128)(2,1)S(1)} %collective-permute-done.7.refs_2_, ...), custom_call_target="tpu_custom_call" | custom-call | flops 8589934592 | bytes 13631488 | tf_op jit(solution)/shard_map/pallas_call | solution.py:75
  187.9 15.3 %shard_map.49 = bf16[64,8192]{1,0:T(8,128)(2,1)S(1)} custom-call(s32[1024]{0:T(1024)S(1)} %fusion.12.src_ref, bf16[64,8192]{1,0:T(8,128)(2,1)S(1)} %bitcast.44, bf16[64,8192]{1,0:T(8,128)(2,1)S(1)} %collective-permute-done.15.refs_1_, bf16[32,8192]{1,0:T(8,128)(2,1)S(1)} %collective-permute-done.17.refs_2_, ...), custom_call_target="tpu_custom_call" | custom-call | flops 8589934592 | bytes 13631488 | tf_op jit(solution)/shard_map/pallas_call | solution.py:75
  203.2 2.0 collective-permute-start.19
  205.3 0.1 collective-permute-done.9
  205.4 15.4 %collective-permute-done.19 = bf16[64,8192]{1,0:T(8,128)(2,1)S(1)} collective-permute-done((bf16[64,8192]{1,0:T(8,128)(2,1)S(1)}, bf16[64,8192]{1,0:T(8,128)(2,1)S(1)}, u32[]{:S(2)}, u32[]{:S(2)}) %collective-permute-start.19) | collective-permute-done | bytes 1048608 | tf_op jit(solution)/shard_map/ppermute | solution.py:17
  220.9 1.5 pad_maximum_fusion
  (36 shorter events, 0.6 us)
Async XLA Ops:
  3.2 25.0 %collective-permute-start.1 = (bf16[64,8192]{1,0:T(8,128)(2,1)S(1)}, bf16[64,8192]{1,0:T(8,128)(2,1)S(1)}, u32[]{:S(2)}, u32[]{:S(2)}) collective-permute-start(bf16[64,8192]{1,0:T(8,128)(2,1)S(1)} %bitcast.39), channel_id=1, source_target_pairs={{0,1},{1,2},{2,3},{3,0},{4,5},{5,6},{6,7},{7,4},{8,9},{9,10},{10,1... | collective-permute-start | bytes 3145736 | tf_op jit(solution)/shard_map/ppermute | solution.py:17
  5.5 24.3 %collective-permute-start = (bf16[64,8192]{1,0:T(8,128)(2,1)S(1)}, bf16[64,8192]{1,0:T(8,128)(2,1)S(1)}, u32[]{:S(2)}, u32[]{:S(2)}) collective-permute-start(bf16[64,8192]{1,0:T(8,128)(2,1)S(1)} %bitcast.40), channel_id=1, source_target_pairs={{0,3},{1,0},{2,1},{3,2},{4,7},{5,4},{6,5},{7,6},{8,11},{9,8},{10,9... | collective-permute-start | bytes 3145736 | tf_op jit(solution)/shard_map/ppermute | solution.py:17
  28.2 12.9 %collective-permute-start.2 = (bf16[32,8192]{1,0:T(8,128)(2,1)S(1)}, bf16[32,8192]{1,0:T(8,128)(2,1)S(1)}, u32[]{:S(2)}, u32[]{:S(2)}) collective-permute-start(bf16[32,8192]{1,0:T(8,128)(2,1)S(1)} %slice.40), channel_id=1, source_target_pairs={{0,1},{1,2},{2,3},{3,0},{4,5},{5,6},{6,7},{7,4},{8,9},{9,10},{10,1... | collective-permute-start | bytes 1572872 | tf_op jit(solution)/shard_map/ppermute | solution.py:17
  29.8 1.4 copy-start
  29.8 12.6 %collective-permute-start.3 = (bf16[32,8192]{1,0:T(8,128)(2,1)S(1)}, bf16[32,8192]{1,0:T(8,128)(2,1)S(1)}, u32[]{:S(2)}, u32[]{:S(2)}) collective-permute-start(bf16[32,8192]{1,0:T(8,128)(2,1)S(1)} %slice.41), channel_id=1, source_target_pairs={{0,3},{1,0},{2,1},{3,2},{4,7},{5,4},{6,5},{7,6},{8,11},{9,8},{10,9... | collective-permute-start | bytes 1572872 | tf_op jit(solution)/shard_map/ppermute | solution.py:17
  30.7 15.2 %copy-start.6 = (s32[1,128,8]{1,2,0:T(8,128)S(1)}, s32[1,128,8]{1,2,0:T(8,128)}, u32[]{:S(2)}) copy-start(s32[1,128,8]{1,2,0:T(8,128)} %param.6) | copy-start | bytes 12292
  41.1 0.8 copy-start.2
  42.4 0.8 copy-start.4
  43.2 22.6 %collective-permute-start.11 = (bf16[64,8192]{1,0:T(8,128)(2,1)S(1)}, bf16[64,8192]{1,0:T(8,128)(2,1)}, u32[]{:S(2)}, u32[]{:S(2)}) collective-permute-start(bf16[64,8192]{1,0:T(8,128)(2,1)S(1)} %bitcast.48), channel_id=1, source_target_pairs={{0,1},{1,2},{2,3},{3,0},{4,5},{5,6},{6,7},{7,4},{8,9},{9,10},{10,1... | collective-permute-start | bytes 3145736 | tf_op jit(solution)/shard_map/ppermute | solution.py:17
  44.2 24.4 %collective-permute-start.10 = (bf16[64,8192]{1,0:T(8,128)(2,1)S(1)}, bf16[64,8192]{1,0:T(8,128)(2,1)}, u32[]{:S(2)}, u32[]{:S(2)}) collective-permute-start(bf16[64,8192]{1,0:T(8,128)(2,1)S(1)} %bitcast.49), channel_id=1, source_target_pairs={{0,3},{1,0},{2,1},{3,2},{4,7},{5,4},{6,5},{7,6},{8,11},{9,8},{10,9... | collective-permute-start | bytes 3145736 | tf_op jit(solution)/shard_map/ppermute | solution.py:17
  46.1 24.3 %copy-start.1 = (bf16[64,8192]{1,0:T(8,128)(2,1)S(1)}, bf16[64,8192]{1,0:T(8,128)(2,1)}, u32[]{:S(2)}) copy-start(bf16[64,8192]{1,0:T(8,128)(2,1)} %copy-done) | copy-start | bytes 3145732
  46.1 24.3 %copy-start.3 = (bf16[32,8192]{1,0:T(8,128)(2,1)S(1)}, bf16[32,8192]{1,0:T(8,128)(2,1)}, u32[]{:S(2)}) copy-start(bf16[32,8192]{1,0:T(8,128)(2,1)} %copy-done.2) | copy-start | bytes 1572868
  46.1 24.3 %copy-start.5 = (bf16[32,8192]{1,0:T(8,128)(2,1)S(1)}, bf16[32,8192]{1,0:T(8,128)(2,1)}, u32[]{:S(2)}) copy-start(bf16[32,8192]{1,0:T(8,128)(2,1)} %copy-done.4) | copy-start | bytes 1572868
  67.0 18.9 %collective-permute-start.12 = (bf16[32,8192]{1,0:T(8,128)(2,1)S(1)}, bf16[32,8192]{1,0:T(8,128)(2,1)S(1)}, u32[]{:S(2)}, u32[]{:S(2)}) collective-permute-start(bf16[32,8192]{1,0:T(8,128)(2,1)S(1)} %slice.44), channel_id=1, source_target_pairs={{0,1},{1,2},{2,3},{3,0},{4,5},{5,6},{6,7},{7,4},{8,9},{9,10},{10,1... | collective-permute-start | bytes 1572872 | tf_op jit(solution)/shard_map/ppermute | solution.py:17
  69.6 16.2 %collective-permute-start.13 = (bf16[32,8192]{1,0:T(8,128)(2,1)S(1)}, bf16[32,8192]{1,0:T(8,128)(2,1)S(1)}, u32[]{:S(2)}, u32[]{:S(2)}) collective-permute-start(bf16[32,8192]{1,0:T(8,128)(2,1)S(1)} %slice.45), channel_id=1, source_target_pairs={{0,3},{1,0},{2,1},{3,2},{4,7},{5,4},{6,5},{7,6},{8,11},{9,8},{10,9... | collective-permute-start | bytes 1572872 | tf_op jit(solution)/shard_map/ppermute | solution.py:17
  85.7 21.0 %collective-permute-start.4 = (bf16[64,8192]{1,0:T(8,128)(2,1)S(1)}, bf16[64,8192]{1,0:T(8,128)(2,1)S(1)}, u32[]{:S(2)}, u32[]{:S(2)}) collective-permute-start(bf16[64,8192]{1,0:T(8,128)(2,1)S(1)} %shard_map.46), channel_id=1, source_target_pairs={{0,4},{4,8},{8,12},{12,16},{16,20},{20,24},{24,28},{28,32},{32,36}... | collective-permute-start | bytes 3145736 | tf_op jit(solution)/shard_map/ppermute | solution.py:17
  102.6 19.4 %collective-permute-start.14 = (bf16[64,8192]{1,0:T(8,128)(2,1)S(1)}, bf16[64,8192]{1,0:T(8,128)(2,1)S(1)}, u32[]{:S(2)}, u32[]{:S(2)}) collective-permute-start(bf16[64,8192]{1,0:T(8,128)(2,1)S(1)} %shard_map.48), channel_id=1, source_target_pairs={{0,4},{4,8},{8,12},{12,16},{16,20},{20,24},{24,28},{28,32},{32,36}... | collective-permute-start | bytes 3145736 | tf_op jit(solution)/shard_map/ppermute | solution.py:17
  108.2 26.8 %collective-permute-start.6 = (bf16[64,8192]{1,0:T(8,128)(2,1)S(1)}, bf16[64,8192]{1,0:T(8,128)(2,1)S(1)}, u32[]{:S(2)}, u32[]{:S(2)}) collective-permute-start(bf16[64,8192]{1,0:T(8,128)(2,1)S(1)} %bitcast.45), channel_id=1, source_target_pairs={{0,1},{1,2},{2,3},{3,0},{4,5},{5,6},{6,7},{7,4},{8,9},{9,10},{10,1... | collective-permute-start | bytes 3145736 | tf_op jit(solution)/shard_map/ppermute | solution.py:17
  111.5 27.3 %collective-permute-start.5 = (bf16[64,8192]{1,0:T(8,128)(2,1)S(1)}, bf16[64,8192]{1,0:T(8,128)(2,1)S(1)}, u32[]{:S(2)}, u32[]{:S(2)}) collective-permute-start(bf16[64,8192]{1,0:T(8,128)(2,1)S(1)} %bitcast.46), channel_id=1, source_target_pairs={{0,3},{1,0},{2,1},{3,2},{4,7},{5,4},{6,5},{7,6},{8,11},{9,8},{10,9... | collective-permute-start | bytes 3145736 | tf_op jit(solution)/shard_map/ppermute | solution.py:17
  123.5 34.0 %collective-permute-start.16 = (bf16[64,8192]{1,0:T(8,128)(2,1)S(1)}, bf16[64,8192]{1,0:T(8,128)(2,1)S(1)}, u32[]{:S(2)}, u32[]{:S(2)}) collective-permute-start(bf16[64,8192]{1,0:T(8,128)(2,1)S(1)} %bitcast.42), channel_id=1, source_target_pairs={{0,1},{1,2},{2,3},{3,0},{4,5},{5,6},{6,7},{7,4},{8,9},{9,10},{10,1... | collective-permute-start | bytes 3145736 | tf_op jit(solution)/shard_map/ppermute | solution.py:17
  126.7 34.7 %collective-permute-start.15 = (bf16[64,8192]{1,0:T(8,128)(2,1)S(1)}, bf16[64,8192]{1,0:T(8,128)(2,1)S(1)}, u32[]{:S(2)}, u32[]{:S(2)}) collective-permute-start(bf16[64,8192]{1,0:T(8,128)(2,1)S(1)} %bitcast.43), channel_id=1, source_target_pairs={{0,3},{1,0},{2,1},{3,2},{4,7},{5,4},{6,5},{7,6},{8,11},{9,8},{10,9... | collective-permute-start | bytes 3145736 | tf_op jit(solution)/shard_map/ppermute | solution.py:17
  135.1 33.7 %collective-permute-start.7 = (bf16[32,8192]{1,0:T(8,128)(2,1)S(1)}, bf16[32,8192]{1,0:T(8,128)(2,1)S(1)}, u32[]{:S(2)}, u32[]{:S(2)}) collective-permute-start(bf16[32,8192]{1,0:T(8,128)(2,1)S(1)} %slice.42), channel_id=1, source_target_pairs={{0,1},{1,2},{2,3},{3,0},{4,5},{5,6},{6,7},{7,4},{8,9},{9,10},{10,1... | collective-permute-start | bytes 1572872 | tf_op jit(solution)/shard_map/ppermute | solution.py:17
  138.9 33.6 %collective-permute-start.8 = (bf16[32,8192]{1,0:T(8,128)(2,1)S(1)}, bf16[32,8192]{1,0:T(8,128)(2,1)S(1)}, u32[]{:S(2)}, u32[]{:S(2)}) collective-permute-start(bf16[32,8192]{1,0:T(8,128)(2,1)S(1)} %slice.43), channel_id=1, source_target_pairs={{0,3},{1,0},{2,1},{3,2},{4,7},{5,4},{6,5},{7,6},{8,11},{9,8},{10,9... | collective-permute-start | bytes 1572872 | tf_op jit(solution)/shard_map/ppermute | solution.py:17
  157.6 30.3 %collective-permute-start.17 = (bf16[32,8192]{1,0:T(8,128)(2,1)S(1)}, bf16[32,8192]{1,0:T(8,128)(2,1)S(1)}, u32[]{:S(2)}, u32[]{:S(2)}) collective-permute-start(bf16[32,8192]{1,0:T(8,128)(2,1)S(1)} %slice.46), channel_id=1, source_target_pairs={{0,1},{1,2},{2,3},{3,0},{4,5},{5,6},{6,7},{7,4},{8,9},{9,10},{10,1... | collective-permute-start | bytes 1572872 | tf_op jit(solution)/shard_map/ppermute | solution.py:17
  161.4 26.5 %collective-permute-start.18 = (bf16[32,8192]{1,0:T(8,128)(2,1)S(1)}, bf16[32,8192]{1,0:T(8,128)(2,1)S(1)}, u32[]{:S(2)}, u32[]{:S(2)}) collective-permute-start(bf16[32,8192]{1,0:T(8,128)(2,1)S(1)} %slice.47), channel_id=1, source_target_pairs={{0,3},{1,0},{2,1},{3,2},{4,7},{5,4},{6,5},{7,6},{8,11},{9,8},{10,9... | collective-permute-start | bytes 1572872 | tf_op jit(solution)/shard_map/ppermute | solution.py:17
  187.8 17.6 %collective-permute-start.9 = (bf16[64,8192]{1,0:T(8,128)(2,1)S(1)}, bf16[64,8192]{1,0:T(8,128)(2,1)S(1)}, u32[]{:S(2)}, u32[]{:S(2)}) collective-permute-start(bf16[64,8192]{1,0:T(8,128)(2,1)S(1)} %shard_map.47), channel_id=1, source_target_pairs={{0,4},{4,8},{8,12},{12,16},{16,20},{20,24},{24,28},{28,32},{32,36}... | collective-permute-start | bytes 3145736 | tf_op jit(solution)/shard_map/ppermute | solution.py:17
  203.2 17.6 %collective-permute-start.19 = (bf16[64,8192]{1,0:T(8,128)(2,1)S(1)}, bf16[64,8192]{1,0:T(8,128)(2,1)S(1)}, u32[]{:S(2)}, u32[]{:S(2)}) collective-permute-start(bf16[64,8192]{1,0:T(8,128)(2,1)S(1)} %shard_map.49), channel_id=1, source_target_pairs={{0,4},{4,8},{8,12},{12,16},{16,20},{20,24},{24,28},{28,32},{32,36}... | collective-permute-start | bytes 3145736 | tf_op jit(solution)/shard_map/ppermute | solution.py:17

commit v5 on v3

--- a/solution.py
+++ b/solution.py
@@ -52,9 +52,7 @@
                 s = src_ref[j * fanin + 2 * m + h]
                 start = pl.multiple_of((s // 2) * (2 * BLK), 2 * BLK)
                 x = x_ref[:, pl.ds(start, 2 * BLK)]
-                swapped = pltpu.roll(x, BLK, 1)
-                keep = (s % 2) == h
-                halves.append(jnp.where(keep, x, swapped))
+                halves.append(pltpu.roll(x, ((s + h) % 2) * BLK, 1))
             pairs.append(jnp.where(lane < BLK, halves[0], halves[1]))
         a = jnp.concatenate(pairs, axis=1)
         tiles = w_ref[jj].reshape(fanin, BLK // 2, 2 * BLK)

time: 213 us -> 210 us (0.986)
  Pallas kernels: 63.5 us -> 58.4 us
    pallas_call x4, Pallas kernels: 63.5 us -> 58.4 us  [block_layer(): pl.pallas_call(functools.partial(product_kernel, fanin), grid_spec=pltpu....]
    ppermute x20, waiting for transfers between devices: 113 us -> 115 us  [from_behind(): lax.ppermute(array, axis, [(i, (i + by) % size) for i in range(size)])]
  transfers between devices with their start and end apart: 20 -> 20, of which waited for: 12 -> 12; matrix products, arithmetic and copies ran while one was open for 4% -> 4% of each run, Pallas kernels for 30% -> 28%
where the time goes in v5:
time: 210 us
  waiting for transfers between devices  115 us (55%)
  Pallas kernels  58.4 us (28%)
  starting transfers between devices  22.3 us (11%)
  local copies, waits for them, and re-layouts  9.02 us (4%)
    ppermute x20, waiting for transfers between devices, from_behind(): lax.ppermute(array, axis, [(i, (i + by) % size) for i in range(size)])  115 us
    pallas_call x4, Pallas kernels, block_layer(): pl.pallas_call(functools.partial(product_kernel, fanin), grid_spec=pltpu....  58.4 us
    ppermute x20, starting transfers between devices, from_behind(): lax.ppermute(array, axis, [(i, (i + by) % size) for i in range(size)])  22.3 us
    unnamed x20, local copies, waits for them, and re-layouts  5.9 us
  transfers between devices with their start and end apart: 20, of which 12 were waited for; matrix products, arithmetic and copies ran while one was open for 4% of the time, Pallas kernels for 28%

profile of v5, /device:TPU:6, one launch (start us, length us, event | category | flops | bytes accessed | tf_op | source)
XLA Modules:
  0.0 209.6 jit_solution(3585972615938584489)
XLA Ops:
  0.0 1.7 slice_bitcast_fusion.1
  1.7 0.3 copy.10
  2.0 0.5 convolution_convert_fusion.1
  2.5 0.7 copy.19
  3.2 2.3 %collective-permute-start.11 = (bf16[64,8192]{1,0:T(8,128)(2,1)S(1)}, bf16[64,8192]{1,0:T(8,128)(2,1)S(1)}, u32[]{:S(2)}, u32[]{:S(2)}) collective-permute-start(bf16[64,8192]{1,0:T(8,128)(2,1)S(1)} %bitcast.42), channel_id=1, source_target_pairs={{0,1},{1,2},{2,3},{3,0},{4,5},{5,6},{6,7},{7,4},{8,9},{9,10},{10,1... | collective-permute-start | bytes 3145736 | tf_op jit(solution)/shard_map/ppermute | solution.py:17
  5.5 0.3 copy.6
  5.8 0.5 convolution_convert_fusion.3
  6.3 0.7 copy.21
  7.0 3.3 %collective-permute-start.1 = (bf16[64,8192]{1,0:T(8,128)(2,1)S(1)}, bf16[64,8192]{1,0:T(8,128)(2,1)S(1)}, u32[]{:S(2)}, u32[]{:S(2)}) collective-permute-start(bf16[64,8192]{1,0:T(8,128)(2,1)S(1)} %bitcast.39), channel_id=1, source_target_pairs={{0,1},{1,2},{2,3},{3,0},{4,5},{5,6},{6,7},{7,4},{8,9},{9,10},{10,1... | collective-permute-start | bytes 3145736 | tf_op jit(solution)/shard_map/ppermute | solution.py:17
  10.3 19.0 %collective-permute-done.11.refs_4_ = bf16[64,8192]{1,0:T(8,128)(2,1)S(1)} collective-permute-done((bf16[64,8192]{1,0:T(8,128)(2,1)S(1)}, bf16[64,8192]{1,0:T(8,128)(2,1)S(1)}, u32[]{:S(2)}, u32[]{:S(2)}) %collective-permute-start.11) | collective-permute-done | bytes 1048608 | tf_op jit(solution)/shard_map/ppermute | solution.py:17
  29.3 0.9 slice.44
  30.2 3.5 %collective-permute-start.12 = (bf16[32,8192]{1,0:T(8,128)(2,1)}, bf16[32,8192]{1,0:T(8,128)(2,1)}, u32[]{:S(2)}, u32[]{:S(2)}) collective-permute-start(bf16[32,8192]{1,0:T(8,128)(2,1)} %slice.44), channel_id=1, source_target_pairs={{0,1},{1,2},{2,3},{3,0},{4,5},{5,6},{6,7},{7,4},{8,9},{9,10},{10,1... | collective-permute-start | bytes 1572872 | tf_op jit(solution)/shard_map/ppermute | solution.py:17
  33.7 0.9 slice.45
  34.6 0.3 copy-done.2
  35.5 0.1 copy.5
  35.7 16.1 %collective-permute-done.1.refs_4_ = bf16[64,8192]{1,0:T(8,128)(2,1)S(1)} collective-permute-done((bf16[64,8192]{1,0:T(8,128)(2,1)S(1)}, bf16[64,8192]{1,0:T(8,128)(2,1)S(1)}, u32[]{:S(2)}, u32[]{:S(2)}) %collective-permute-start.1) | collective-permute-done | bytes 1048608 | tf_op jit(solution)/shard_map/ppermute | solution.py:17
  51.8 3.5 %collective-permute-start.2 = (bf16[32,8192]{1,0:T(8,128)(2,1)S(1)}, bf16[32,8192]{1,0:T(8,128)(2,1)S(1)}, u32[]{:S(2)}, u32[]{:S(2)}) collective-permute-start(bf16[32,8192]{1,0:T(8,128)(2,1)S(1)} %slice.40), channel_id=1, source_target_pairs={{0,1},{1,2},{2,3},{3,0},{4,5},{5,6},{6,7},{7,4},{8,9},{9,10},{10,1... | collective-permute-start | bytes 1572872 | tf_op jit(solution)/shard_map/ppermute | solution.py:17
  55.4 1.1 slice.41
  56.5 6.6 %collective-permute-done.12.refs_2_ = bf16[32,8192]{1,0:T(8,128)(2,1)} collective-permute-done((bf16[32,8192]{1,0:T(8,128)(2,1)}, bf16[32,8192]{1,0:T(8,128)(2,1)}, u32[]{:S(2)}, u32[]{:S(2)}) %collective-permute-start.12) | collective-permute-done | bytes 524320 | tf_op jit(solution)/shard_map/ppermute | solution.py:17
  63.1 3.5 %collective-permute-done.13.refs_3_ = bf16[32,8192]{1,0:T(8,128)(2,1)} collective-permute-done((bf16[32,8192]{1,0:T(8,128)(2,1)}, bf16[32,8192]{1,0:T(8,128)(2,1)}, u32[]{:S(2)}, u32[]{:S(2)}) %collective-permute-start.13) | collective-permute-done | bytes 524320 | tf_op jit(solution)/shard_map/ppermute | solution.py:17
  66.6 15.2 %shard_map.48 = bf16[64,8192]{1,0:T(8,128)(2,1)S(1)} custom-call(s32[1024]{0:T(1024)S(1)} %fusion.12.src_ref, bf16[64,8192]{1,0:T(8,128)(2,1)S(1)} %bitcast.44, bf16[64,8192]{1,0:T(8,128)(2,1)S(1)} %copy-done.3, bf16[32,8192]{1,0:T(8,128)(2,1)} %collective-permute-done.12.refs_2_, bf16[32,8192]{1,0:T(8,128)(2,1)} %collective-permute-done.13.refs_3_, ...), custom_call_target="tpu_custom_call" | custom-call | flops 8589934592 | bytes 13631488 | tf_op jit(solution)/shard_map/pallas_call | solution.py:73
  81.8 0.3 collective-permute-start.14
  82.1 15.2 %shard_map.46 = bf16[64,8192]{1,0:T(8,128)(2,1)S(1)} custom-call(s32[1024]{0:T(1024)S(1)} %fusion.12.src_ref, bf16[64,8192]{1,0:T(8,128)(2,1)S(1)} %bitcast.41, bf16[64,8192]{1,0:T(8,128)(2,1)} %collective-permute-done.refs_1_, bf16[32,8192]{1,0:T(8,128)(2,1)S(1)} %collective-permute-done.2.refs_2_, bf16[32,8192]{1,0:T(8,128)(2,1)S(1)} %collective-permute-done.3.refs_3_, ...), custom_call_target="tpu_custom_call" | custom-call | flops 8589934592 | bytes 13631488 | tf_op jit(solution)/shard_map/pallas_call | solution.py:73
  97.3 0.3 collective-permute-start.4
  97.6 2.0 collective-permute-done.14
  99.6 0.3 copy.12
  99.9 0.5 convolution_convert_fusion
  100.4 0.7 copy.18
  101.2 2.0 collective-permute-start.15
  103.2 11.7 %collective-permute-done.4 = bf16[64,8192]{1,0:T(8,128)(2,1)S(1)} collective-permute-done((bf16[64,8192]{1,0:T(8,128)(2,1)S(1)}, bf16[64,8192]{1,0:T(8,128)(2,1)S(1)}, u32[]{:S(2)}, u32[]{:S(2)}) %collective-permute-start.4) | collective-permute-done | bytes 1048608 | tf_op jit(solution)/shard_map/ppermute | solution.py:17
  114.9 0.3 copy.8
  115.2 0.5 convolution_convert_fusion.2
  115.7 0.7 copy.20
  116.5 2.0 collective-permute-start.5
  118.5 8.8 %collective-permute-done.16.refs_4_ = bf16[64,8192]{1,0:T(8,128)(2,1)S(1)} collective-permute-done((bf16[64,8192]{1,0:T(8,128)(2,1)S(1)}, bf16[64,8192]{1,0:T(8,128)(2,1)S(1)}, u32[]{:S(2)}, u32[]{:S(2)}) %collective-permute-start.16) | collective-permute-done | bytes 1048608 | tf_op jit(solution)/shard_map/ppermute | solution.py:17
  127.3 1.3 collective-permute-start.17
  128.6 0.9 collective-permute-start.18
  129.5 20.2 %collective-permute-done.6.refs_4_ = bf16[64,8192]{1,0:T(8,128)(2,1)S(1)} collective-permute-done((bf16[64,8192]{1,0:T(8,128)(2,1)S(1)}, bf16[64,8192]{1,0:T(8,128)(2,1)S(1)}, u32[]{:S(2)}, u32[]{:S(2)}) %collective-permute-start.6) | collective-permute-done | bytes 1048608 | tf_op jit(solution)/shard_map/ppermute | solution.py:17
  149.8 1.3 collective-permute-start.7
  151.1 1.1 collective-permute-start.8
  152.2 8.8 %collective-permute-done.17.refs_2_ = bf16[32,8192]{1,0:T(8,128)(2,1)S(1)} collective-permute-done((bf16[32,8192]{1,0:T(8,128)(2,1)S(1)}, bf16[32,8192]{1,0:T(8,128)(2,1)S(1)}, u32[]{:S(2)}, u32[]{:S(2)}) %collective-permute-start.17) | collective-permute-done | bytes 524320 | tf_op jit(solution)/shard_map/ppermute | solution.py:17
  161.0 1.3 collective-permute-done.18.refs_3_
  162.3 14.0 %shard_map.49 = bf16[64,8192]{1,0:T(8,128)(2,1)S(1)} custom-call(s32[1024]{0:T(1024)S(1)} %fusion.12.src_ref, bf16[64,8192]{1,0:T(8,128)(2,1)S(1)} %bitcast.50, bf16[64,8192]{1,0:T(8,128)(2,1)S(1)} %collective-permute-done.15.refs_1_, bf16[32,8192]{1,0:T(8,128)(2,1)S(1)} %collective-permute-done.17.refs_2_, ...), custom_call_target="tpu_custom_call" | custom-call | flops 8589934592 | bytes 13631488 | tf_op jit(solution)/shard_map/pallas_call | solution.py:73
  176.4 14.0 %shard_map.47 = bf16[64,8192]{1,0:T(8,128)(2,1)S(1)} custom-call(s32[1024]{0:T(1024)S(1)} %fusion.12.src_ref, bf16[64,8192]{1,0:T(8,128)(2,1)S(1)} %bitcast.47, bf16[64,8192]{1,0:T(8,128)(2,1)S(1)} %collective-permute-done.5.refs_1_, bf16[32,8192]{1,0:T(8,128)(2,1)S(1)} %collective-permute-done.7.refs_2_, ...), custom_call_target="tpu_custom_call" | custom-call | flops 8589934592 | bytes 13631488 | tf_op jit(solution)/shard_map/pallas_call | solution.py:73
  190.4 0.2 collective-permute-start.9
  190.7 3.3 %collective-permute-done.19 = bf16[64,8192]{1,0:T(8,128)(2,1)S(1)} collective-permute-done((bf16[64,8192]{1,0:T(8,128)(2,1)S(1)}, bf16[64,8192]{1,0:T(8,128)(2,1)S(1)}, u32[]{:S(2)}, u32[]{:S(2)}) %collective-permute-start.19) | collective-permute-done | bytes 1048608 | tf_op jit(solution)/shard_map/ppermute | solution.py:17
  193.9 14.2 %collective-permute-done.9 = bf16[64,8192]{1,0:T(8,128)(2,1)S(1)} collective-permute-done((bf16[64,8192]{1,0:T(8,128)(2,1)S(1)}, bf16[64,8192]{1,0:T(8,128)(2,1)S(1)}, u32[]{:S(2)}, u32[]{:S(2)}) %collective-permute-start.9) | collective-permute-done | bytes 1048608 | tf_op jit(solution)/shard_map/ppermute | solution.py:17
  208.1 1.5 pad_maximum_fusion
  (32 shorter events, 0.7 us)
Async XLA Ops:
  3.2 26.1 %collective-permute-start.11 = (bf16[64,8192]{1,0:T(8,128)(2,1)S(1)}, bf16[64,8192]{1,0:T(8,128)(2,1)S(1)}, u32[]{:S(2)}, u32[]{:S(2)}) collective-permute-start(bf16[64,8192]{1,0:T(8,128)(2,1)S(1)} %bitcast.42), channel_id=1, source_target_pairs={{0,1},{1,2},{2,3},{3,0},{4,5},{5,6},{6,7},{7,4},{8,9},{9,10},{10,1... | collective-permute-start | bytes 3145736 | tf_op jit(solution)/shard_map/ppermute | solution.py:17
  5.5 28.2 %collective-permute-start.10 = (bf16[64,8192]{1,0:T(8,128)(2,1)S(1)}, bf16[64,8192]{1,0:T(8,128)(2,1)S(1)}, u32[]{:S(2)}, u32[]{:S(2)}) collective-permute-start(bf16[64,8192]{1,0:T(8,128)(2,1)S(1)} %bitcast.43), channel_id=1, source_target_pairs={{0,3},{1,0},{2,1},{3,2},{4,7},{5,4},{6,5},{7,6},{8,11},{9,8},{10,9... | collective-permute-start | bytes 3145736 | tf_op jit(solution)/shard_map/ppermute | solution.py:17
  6.3 29.2 %copy-start.4 = (s32[1,128,8]{1,2,0:T(8,128)S(1)}, s32[1,128,8]{1,2,0:T(8,128)}, u32[]{:S(2)}) copy-start(s32[1,128,8]{1,2,0:T(8,128)} %param.6) | copy-start | bytes 12292
  7.0 44.8 %collective-permute-start.1 = (bf16[64,8192]{1,0:T(8,128)(2,1)S(1)}, bf16[64,8192]{1,0:T(8,128)(2,1)S(1)}, u32[]{:S(2)}, u32[]{:S(2)}) collective-permute-start(bf16[64,8192]{1,0:T(8,128)(2,1)S(1)} %bitcast.39), channel_id=1, source_target_pairs={{0,1},{1,2},{2,3},{3,0},{4,5},{5,6},{6,7},{7,4},{8,9},{9,10},{10,1... | collective-permute-start | bytes 3145736 | tf_op jit(solution)/shard_map/ppermute | solution.py:17
  10.3 45.1 %collective-permute-start = (bf16[64,8192]{1,0:T(8,128)(2,1)S(1)}, bf16[64,8192]{1,0:T(8,128)(2,1)}, u32[]{:S(2)}, u32[]{:S(2)}) collective-permute-start(bf16[64,8192]{1,0:T(8,128)(2,1)S(1)} %bitcast.40), channel_id=1, source_target_pairs={{0,3},{1,0},{2,1},{3,2},{4,7},{5,4},{6,5},{7,6},{8,11},{9,8},{10,9... | collective-permute-start | bytes 3145736 | tf_op jit(solution)/shard_map/ppermute | solution.py:17
  29.3 4.4 %copy-start = (bf16[64,8192]{1,0:T(8,128)(2,1)}, bf16[64,8192]{1,0:T(8,128)(2,1)S(1)}, u32[]{:S(2)}) copy-start(bf16[64,8192]{1,0:T(8,128)(2,1)S(1)} %collective-permute-done.11.refs_4_) | copy-start | bytes 3145732
  30.2 32.9 %collective-permute-start.12 = (bf16[32,8192]{1,0:T(8,128)(2,1)}, bf16[32,8192]{1,0:T(8,128)(2,1)}, u32[]{:S(2)}, u32[]{:S(2)}) collective-permute-start(bf16[32,8192]{1,0:T(8,128)(2,1)} %slice.44), channel_id=1, source_target_pairs={{0,1},{1,2},{2,3},{3,0},{4,5},{5,6},{6,7},{7,4},{8,9},{9,10},{10,1... | collective-permute-start | bytes 1572872 | tf_op jit(solution)/shard_map/ppermute | solution.py:17
  33.7 1.1 copy-start.2
  34.8 31.8 %collective-permute-start.13 = (bf16[32,8192]{1,0:T(8,128)(2,1)}, bf16[32,8192]{1,0:T(8,128)(2,1)}, u32[]{:S(2)}, u32[]{:S(2)}) collective-permute-start(bf16[32,8192]{1,0:T(8,128)(2,1)} %slice.45), channel_id=1, source_target_pairs={{0,3},{1,0},{2,1},{3,2},{4,7},{5,4},{6,5},{7,6},{8,11},{9,8},{10,9... | collective-permute-start | bytes 1572872 | tf_op jit(solution)/shard_map/ppermute | solution.py:17
  35.7 30.9 %copy-start.1 = (bf16[64,8192]{1,0:T(8,128)(2,1)S(1)}, bf16[64,8192]{1,0:T(8,128)(2,1)}, u32[]{:S(2)}) copy-start(bf16[64,8192]{1,0:T(8,128)(2,1)} %copy-done) | copy-start | bytes 3145732
  35.7 30.9 %copy-start.3 = (bf16[64,8192]{1,0:T(8,128)(2,1)S(1)}, bf16[64,8192]{1,0:T(8,128)(2,1)}, u32[]{:S(2)}) copy-start(bf16[64,8192]{1,0:T(8,128)(2,1)} %copy-done.2) | copy-start | bytes 3145732
  51.8 30.3 %collective-permute-start.2 = (bf16[32,8192]{1,0:T(8,128)(2,1)S(1)}, bf16[32,8192]{1,0:T(8,128)(2,1)S(1)}, u32[]{:S(2)}, u32[]{:S(2)}) collective-permute-start(bf16[32,8192]{1,0:T(8,128)(2,1)S(1)} %slice.40), channel_id=1, source_target_pairs={{0,1},{1,2},{2,3},{3,0},{4,5},{5,6},{6,7},{7,4},{8,9},{9,10},{10,1... | collective-permute-start | bytes 1572872 | tf_op jit(solution)/shard_map/ppermute | solution.py:17
  56.5 25.6 %collective-permute-start.3 = (bf16[32,8192]{1,0:T(8,128)(2,1)S(1)}, bf16[32,8192]{1,0:T(8,128)(2,1)S(1)}, u32[]{:S(2)}, u32[]{:S(2)}) collective-permute-start(bf16[32,8192]{1,0:T(8,128)(2,1)S(1)} %slice.41), channel_id=1, source_target_pairs={{0,3},{1,0},{2,1},{3,2},{4,7},{5,4},{6,5},{7,6},{8,11},{9,8},{10,9... | collective-permute-start | bytes 1572872 | tf_op jit(solution)/shard_map/ppermute | solution.py:17
  81.8 17.8 %collective-permute-start.14 = (bf16[64,8192]{1,0:T(8,128)(2,1)S(1)}, bf16[64,8192]{1,0:T(8,128)(2,1)S(1)}, u32[]{:S(2)}, u32[]{:S(2)}) collective-permute-start(bf16[64,8192]{1,0:T(8,128)(2,1)S(1)} %shard_map.48), channel_id=1, source_target_pairs={{0,4},{4,8},{8,12},{12,16},{16,20},{20,24},{24,28},{28,32},{32,36}... | collective-permute-start | bytes 3145736 | tf_op jit(solution)/shard_map/ppermute | solution.py:17
  97.3 17.6 %collective-permute-start.4 = (bf16[64,8192]{1,0:T(8,128)(2,1)S(1)}, bf16[64,8192]{1,0:T(8,128)(2,1)S(1)}, u32[]{:S(2)}, u32[]{:S(2)}) collective-permute-start(bf16[64,8192]{1,0:T(8,128)(2,1)S(1)} %shard_map.46), channel_id=1, source_target_pairs={{0,4},{4,8},{8,12},{12,16},{16,20},{20,24},{24,28},{28,32},{32,36}... | collective-permute-start | bytes 3145736 | tf_op jit(solution)/shard_map/ppermute | solution.py:17
  101.1 26.2 %collective-permute-start.16 = (bf16[64,8192]{1,0:T(8,128)(2,1)S(1)}, bf16[64,8192]{1,0:T(8,128)(2,1)S(1)}, u32[]{:S(2)}, u32[]{:S(2)}) collective-permute-start(bf16[64,8192]{1,0:T(8,128)(2,1)S(1)} %bitcast.48), channel_id=1, source_target_pairs={{0,1},{1,2},{2,3},{3,0},{4,5},{5,6},{6,7},{7,4},{8,9},{9,10},{10,1... | collective-permute-start | bytes 3145736 | tf_op jit(solution)/shard_map/ppermute | solution.py:17
  101.2 27.4 %collective-permute-start.15 = (bf16[64,8192]{1,0:T(8,128)(2,1)S(1)}, bf16[64,8192]{1,0:T(8,128)(2,1)S(1)}, u32[]{:S(2)}, u32[]{:S(2)}) collective-permute-start(bf16[64,8192]{1,0:T(8,128)(2,1)S(1)} %bitcast.49), channel_id=1, source_target_pairs={{0,3},{1,0},{2,1},{3,2},{4,7},{5,4},{6,5},{7,6},{8,11},{9,8},{10,9... | collective-permute-start | bytes 3145736 | tf_op jit(solution)/shard_map/ppermute | solution.py:17
  116.4 33.3 %collective-permute-start.6 = (bf16[64,8192]{1,0:T(8,128)(2,1)S(1)}, bf16[64,8192]{1,0:T(8,128)(2,1)S(1)}, u32[]{:S(2)}, u32[]{:S(2)}) collective-permute-start(bf16[64,8192]{1,0:T(8,128)(2,1)S(1)} %bitcast.45), channel_id=1, source_target_pairs={{0,1},{1,2},{2,3},{3,0},{4,5},{5,6},{6,7},{7,4},{8,9},{9,10},{10,1... | collective-permute-start | bytes 3145736 | tf_op jit(solution)/shard_map/ppermute | solution.py:17
  116.5 34.6 %collective-permute-start.5 = (bf16[64,8192]{1,0:T(8,128)(2,1)S(1)}, bf16[64,8192]{1,0:T(8,128)(2,1)S(1)}, u32[]{:S(2)}, u32[]{:S(2)}) collective-permute-start(bf16[64,8192]{1,0:T(8,128)(2,1)S(1)} %bitcast.46), channel_id=1, source_target_pairs={{0,3},{1,0},{2,1},{3,2},{4,7},{5,4},{6,5},{7,6},{8,11},{9,8},{10,9... | collective-permute-start | bytes 3145736 | tf_op jit(solution)/shard_map/ppermute | solution.py:17
  127.3 33.7 %collective-permute-start.17 = (bf16[32,8192]{1,0:T(8,128)(2,1)S(1)}, bf16[32,8192]{1,0:T(8,128)(2,1)S(1)}, u32[]{:S(2)}, u32[]{:S(2)}) collective-permute-start(bf16[32,8192]{1,0:T(8,128)(2,1)S(1)} %slice.46), channel_id=1, source_target_pairs={{0,1},{1,2},{2,3},{3,0},{4,5},{5,6},{6,7},{7,4},{8,9},{9,10},{10,1... | collective-permute-start | bytes 1572872 | tf_op jit(solution)/shard_map/ppermute | solution.py:17
  128.6 33.6 %collective-permute-start.18 = (bf16[32,8192]{1,0:T(8,128)(2,1)S(1)}, bf16[32,8192]{1,0:T(8,128)(2,1)S(1)}, u32[]{:S(2)}, u32[]{:S(2)}) collective-permute-start(bf16[32,8192]{1,0:T(8,128)(2,1)S(1)} %slice.47), channel_id=1, source_target_pairs={{0,3},{1,0},{2,1},{3,2},{4,7},{5,4},{6,5},{7,6},{8,11},{9,8},{10,9... | collective-permute-start | bytes 1572872 | tf_op jit(solution)/shard_map/ppermute | solution.py:17
  149.8 26.6 %collective-permute-start.7 = (bf16[32,8192]{1,0:T(8,128)(2,1)S(1)}, bf16[32,8192]{1,0:T(8,128)(2,1)S(1)}, u32[]{:S(2)}, u32[]{:S(2)}) collective-permute-start(bf16[32,8192]{1,0:T(8,128)(2,1)S(1)} %slice.42), channel_id=1, source_target_pairs={{0,1},{1,2},{2,3},{3,0},{4,5},{5,6},{6,7},{7,4},{8,9},{9,10},{10,1... | collective-permute-start | bytes 1572872 | tf_op jit(solution)/shard_map/ppermute | solution.py:17
  151.1 25.3 %collective-permute-start.8 = (bf16[32,8192]{1,0:T(8,128)(2,1)S(1)}, bf16[32,8192]{1,0:T(8,128)(2,1)S(1)}, u32[]{:S(2)}, u32[]{:S(2)}) collective-permute-start(bf16[32,8192]{1,0:T(8,128)(2,1)S(1)} %slice.43), channel_id=1, source_target_pairs={{0,3},{1,0},{2,1},{3,2},{4,7},{5,4},{6,5},{7,6},{8,11},{9,8},{10,9... | collective-permute-start | bytes 1572872 | tf_op jit(solution)/shard_map/ppermute | solution.py:17
  176.3 17.6 %collective-permute-start.19 = (bf16[64,8192]{1,0:T(8,128)(2,1)S(1)}, bf16[64,8192]{1,0:T(8,128)(2,1)S(1)}, u32[]{:S(2)}, u32[]{:S(2)}) collective-permute-start(bf16[64,8192]{1,0:T(8,128)(2,1)S(1)} %shard_map.49), channel_id=1, source_target_pairs={{0,4},{4,8},{8,12},{12,16},{16,20},{20,24},{24,28},{28,32},{32,36}... | collective-permute-start | bytes 3145736 | tf_op jit(solution)/shard_map/ppermute | solution.py:17
  190.4 17.6 %collective-permute-start.9 = (bf16[64,8192]{1,0:T(8,128)(2,1)S(1)}, bf16[64,8192]{1,0:T(8,128)(2,1)S(1)}, u32[]{:S(2)}, u32[]{:S(2)}) collective-permute-start(bf16[64,8192]{1,0:T(8,128)(2,1)S(1)} %shard_map.47), channel_id=1, source_target_pairs={{0,4},{4,8},{8,12},{12,16},{16,20},{20,24},{24,28},{28,32},{32,36}... | collective-permute-start | bytes 3145736 | tf_op jit(solution)/shard_map/ppermute | solution.py:17
